TPU v7x, 32 devices: a whole 2x2x4 slice. The times are simulated.
32 devices in a mesh: slab: 8 (over z, x), pencil: 4 (over y, core).
Axes of the slice: x: 2, y: 2, z: 4, core: 2. Of those that a mesh axis runs over, the one named last changes fastest.
Arguments:
- atom_cell: int32 [3, 262144], P(None, ('slab', 'pencil')), may hold values from 0 to 511, as said below
- charge: float32 [262144], P(('slab', 'pencil')), may hold values from -4 to 4
Outputs:
- potential: float32 [64, 128, 512], P('slab', 'pencil')
- forces: float32 [3, 262144], P(None, ('slab', 'pencil'))
Inputs may be any that keep to these rules, and one draw needn't show every extreme that they name: `atom_cell`: the atoms of rows b * 8192 to (b + 1) * 8192 - 1, with b = s * 4 + r, lie in z planes s * 8 to (s + 1) * 8 - 1 and y rows r * 32 to (r + 1) * 32 - 1. Row 0 is at cell (0, 0, 0) and the last row at cell (63, 127, 511).
All inputs are finite; a program needn't handle non-finite values.
Results may differ from a plain program's by a relative error of at most 0.0003.
Values sent between devices are 32-bit elements; how exact they have to be, the bound alone decides.
A program may use at most 128 MiB of HBM per device.

v0:
```python
from functools import partial
import math

import jax
import jax.numpy as jnp
from jax import lax
from jax.sharding import PartitionSpec as P

CZ = 8
CY = 32
NX = 512
LEVELS = 5
RADIUS = 2
F = 32


def extended(cells, sides, width):
    for axis, dim in sides:
        count = lax.axis_size(axis)
        ends = count - 1
        head = lax.slice_in_dim(cells, 0, width, axis=dim)
        tail = lax.slice_in_dim(cells, cells.shape[dim] - width, cells.shape[dim], axis=dim)
        cells = jnp.concatenate(
            [
                lax.ppermute(tail, axis, [(i, (i + 1) % count) for i in range(ends)]),
                cells,
                lax.ppermute(head, axis, [((i + 1) % count, i) for i in range(ends)]),
            ],
            axis=dim,
        )
    return cells


def kernel_weight(step_z, step_y, step_x):
    squared = step_z * step_z + step_y * step_y + step_x * step_x
    return 1.0 / math.sqrt(squared + 0.25) - 1.0 / math.sqrt(squared + 4.0)


def level_weight(scale, step_z, step_y, step_x):
    squared = step_z * step_z + step_y * step_y + step_x * step_x
    return scale * (1.0 / math.sqrt(squared + 1.0) - 1.0 / math.sqrt(squared + 4.0))


def short_field(padded, plane_count, row_count, row_length, radius_cells, weight_of):
    accumulated = jnp.zeros((plane_count, row_count, row_length), jnp.float32)
    for step_z in range(-radius_cells, radius_cells + 1):
        for step_y in range(-radius_cells, radius_cells + 1):
            for step_x in range(-radius_cells, radius_cells + 1):
                corner_z = radius_cells + step_z
                corner_y = radius_cells + step_y
                corner_x = radius_cells + step_x
                accumulated = (
                    accumulated
                    + weight_of(step_z, step_y, step_x)
                    * padded[
                        corner_z : corner_z + plane_count,
                        corner_y : corner_y + row_count,
                        corner_x : corner_x + row_length,
                    ]
                )
    return accumulated


def restrict(grid):
    planes, rows, length = grid.shape
    return grid.reshape(planes // 2, 2, rows // 2, 2, length // 2, 2).sum(axis=(1, 3, 5))


def restrict_plane(plane):
    rows, length = plane.shape
    return plane.reshape(rows // 2, 2, length // 2, 2).sum(axis=(1, 3))


def interp_matrix(fine_ids, level_count, factor, first_col, width):
    numerator = jnp.clip(2 * fine_ids + 1 - factor, 0, 2 * factor * (level_count - 1))
    lower_index = jnp.minimum(numerator // (2 * factor), level_count - 2)
    fraction = (numerator - lower_index * 2 * factor).astype(jnp.float32) / (2.0 * factor)
    local_index = lower_index - first_col
    columns = jnp.arange(width, dtype=jnp.int32)
    low_part = jnp.where(columns[None, :] == local_index[:, None], 1.0 - fraction[:, None], 0.0)
    high_part = jnp.where(columns[None, :] == local_index[:, None] + 1, fraction[:, None], 0.0)
    return low_part + high_part


def to_fine(field, counts, factor, plane_ids, line_ids, column_ids, first_z, first_y):
    width_z, width_y, width_x = field.shape
    along_z = interp_matrix(plane_ids, counts[0], factor, first_z, width_z)
    along_y = interp_matrix(line_ids, counts[1], factor, first_y, width_y)
    along_x = interp_matrix(column_ids, counts[2], factor, 0, width_x)
    section = jnp.einsum("fa,abc->fbc", along_z, field, precision=lax.Precision.HIGHEST)
    section = jnp.einsum("fb,abc->afc", along_y, section, precision=lax.Precision.HIGHEST)
    return jnp.einsum("fc,abc->abf", along_x, section, precision=lax.Precision.HIGHEST)


def top_coords(cell_ids, top_y, top_x):
    return (cell_ids // (top_y * top_x), cell_ids // top_x % top_y, cell_ids % top_x)


def top_potential(targets, charges_flat, top_z, top_y, top_x, strength):
    sources = jnp.arange(top_z * top_y * top_x, dtype=jnp.int32)
    target_xyz = top_coords(targets, top_y, top_x)
    source_xyz = top_coords(sources, top_y, top_x)
    distance = jnp.ones((targets.shape[0], sources.shape[0]), jnp.float32)
    for component in range(3):
        offset = (target_xyz[component][:, None] - source_xyz[component][None, :]).astype(
            jnp.float32
        )
        distance = distance + offset * offset
    kernel = strength / jnp.sqrt(distance)
    return jnp.dot(kernel, charges_flat, precision=lax.Precision.HIGHEST)


def gradient_along(padded, direction, plane_count, row_count, row_length):

    def shifted(offset_cells):
        corner = [2, 2, 2]
        corner[direction] = corner[direction] + offset_cells
        return padded[
            corner[0] : corner[0] + plane_count,
            corner[1] : corner[1] + row_count,
            corner[2] : corner[2] + row_length,
        ]

    return (8.0 * (shifted(1) - shifted(-1)) - (shifted(2) - shifted(-2))) / 12.0


def body(atom_cell, charge):
    slab_pos = lax.axis_index("slab")
    pencil_pos = lax.axis_index("pencil")
    slabs = lax.axis_size("slab")
    pencils = lax.axis_size("pencil")
    atom_total = charge.shape[0]
    row_cells = CZ * CY
    plane_row = (atom_cell[0] - slab_pos * CZ) * CY + (atom_cell[1] - pencil_pos * CY)
    column_of = atom_cell[2]
    block_atoms = math.gcd(atom_total, 512)
    block_count = atom_total // block_atoms
    row_blocks = plane_row.reshape(block_count, block_atoms)
    column_blocks = column_of.reshape(block_count, block_atoms)
    charge_blocks = charge.reshape(block_count, block_atoms)
    row_range = jnp.arange(row_cells, dtype=jnp.int32)
    column_range = jnp.arange(NX, dtype=jnp.int32)

    def deposit(total, block):
        rows_here, columns_here, charges_here = block
        row_table = (rows_here[:, None] == row_range[None, :]).astype(jnp.float32)
        column_table = jnp.where(
            columns_here[:, None] == column_range[None, :], charges_here[:, None], 0.0
        )
        added = jnp.dot(row_table.T, column_table, precision=lax.Precision.HIGHEST)
        return (total + added, None)

    charge_grid, _ = lax.scan(
        deposit, jnp.zeros((row_cells, NX), jnp.float32), (row_blocks, column_blocks, charge_blocks)
    )
    charge_grid = charge_grid.reshape(CZ, CY, NX)
    plane_ids = slab_pos * CZ + jnp.arange(CZ, dtype=jnp.int32)
    line_ids = pencil_pos * CY + jnp.arange(CY, dtype=jnp.int32)
    column_ids = jnp.arange(NX, dtype=jnp.int32)
    plane_level = CZ.bit_length() - 1
    rimmed = extended(charge_grid, (("slab", 0), ("pencil", 1)), RADIUS)
    padded = jnp.pad(rimmed, ((0, 0), (0, 0), (RADIUS, RADIUS)))
    potential = short_field(padded, CZ, CY, NX, RADIUS, kernel_weight)
    level_charge = charge_grid
    for level in range(1, plane_level):
        level_charge = restrict(level_charge)
        level_z, level_y, level_x = level_charge.shape
        cycle = extended(level_charge, (("slab", 0), ("pencil", 1)), RADIUS)
        cycle = jnp.pad(cycle, ((0, 0), (0, 0), (RADIUS, RADIUS)))
        field = short_field(
            cycle, level_z, level_y, level_x, RADIUS, partial(level_weight, 1.0 / 2**level)
        )
        framed = extended(field, (("slab", 0), ("pencil", 1)), 1)
        counts = (level_z * slabs, level_y * pencils, level_x)
        potential = potential + to_fine(
            framed,
            counts,
            2**level,
            plane_ids,
            line_ids,
            column_ids,
            slab_pos * level_z - 1,
            pencil_pos * level_y - 1,
        )
    own_plane = restrict(level_charge)[0]
    pieces = [own_plane]
    partial_plane = own_plane
    for level_bit in range(LEVELS - plane_level):
        partial_plane = restrict_plane(partial_plane)
        pieces.append(partial_plane)
    packed = jnp.concatenate([piece.reshape(1, -1) for piece in pieces], axis=1)
    gathered = lax.all_gather(packed, ("slab", "pencil"), axis=0, tiled=True)
    coarse = []
    offset = 0
    for step, piece in enumerate(pieces):
        rows, length = piece.shape
        group = 2**step
        block = gathered[:, offset : offset + rows * length].reshape(
            slabs // group, group, pencils, rows, length
        )
        grid = block.sum(axis=1)
        coarse.append(grid.reshape(slabs // group, pencils * rows, length))
        offset = offset + rows * length
    for step in range(LEVELS - plane_level):
        level = plane_level + step
        grid = coarse[step]
        level_z, level_y, level_x = grid.shape
        field = short_field(
            jnp.pad(grid, RADIUS),
            level_z,
            level_y,
            level_x,
            RADIUS,
            partial(level_weight, 1.0 / 2**level),
        )
        potential = potential + to_fine(
            field, field.shape, 2**level, plane_ids, line_ids, column_ids, 0, 0
        )
    top_grid = coarse[-1]
    top_z, top_y, top_x = top_grid.shape
    charges_flat = top_grid.reshape(top_z * top_y * top_x)
    top_total = top_z * top_y * top_x
    strength = 1.0 / F
    block_rows = math.gcd(top_total, 512)
    target_blocks = jnp.arange(top_total, dtype=jnp.int32).reshape(
        top_total // block_rows, block_rows
    )
    top_field = lax.map(
        lambda targets: top_potential(targets, charges_flat, top_z, top_y, top_x, strength),
        target_blocks,
    )
    top_field = top_field.reshape(top_z, top_y, top_x)
    potential = potential + to_fine(
        top_field, top_field.shape, F, plane_ids, line_ids, column_ids, 0, 0
    )
    rimmed_field = extended(potential, (("slab", 0), ("pencil", 1)), 2)
    padded_field = jnp.pad(rimmed_field, ((0, 0), (0, 0), (2, 2)))
    gradients = jnp.stack(
        [gradient_along(padded_field, direction, CZ, CY, NX) for direction in range(3)]
    ).reshape(3, row_cells, NX)

    def pick(block):
        rows_here, columns_here, charges_here = block
        row_table = (rows_here[:, None] == row_range[None, :]).astype(jnp.float32)
        column_table = (columns_here[:, None] == column_range[None, :]).astype(jnp.float32)
        picked_rows = jnp.einsum(
            "ar,drx->adx", row_table, gradients, precision=lax.Precision.HIGHEST
        )
        at_cell = jnp.sum(picked_rows * column_table[:, None, :], axis=2)
        return -charges_here[:, None] * at_cell

    picked = lax.map(pick, (row_blocks, column_blocks, charge_blocks))
    forces = picked.reshape(atom_total, 3).T
    return (potential, forces)


def solution(mesh):
    return jax.shard_map(
        body,
        mesh=mesh,
        in_specs=(P(None, ("slab", "pencil")), P(("slab", "pencil"))),
        out_specs=(P("slab", "pencil", None), P(None, ("slab", "pencil"))),
        check_vma=False,
    )
```

profile of v0, /device:TPU:3, one launch (start us, length us, event | category | flops | bytes accessed | tf_op | source)
XLA Modules:
  0.0 269.1 jit_solution(17136791525805690343)
XLA Ops:
  2.7 18.5 %while.27 = (s32[]{:T(128)}, f32[256,512]{1,0:T(8,128)S(1)}, s32[16,512]{1,0:T(8,128)S(1)}, s32[16,512]{1,0:T(8,128)S(1)}, f32[16,512]{1,0:T(8,128)S(1)}, /*index=5*/s32[]{:T(128)}, s32[]{:T(128)}) while((s32[]{:T(128)}, f32[256,512]{1,0:T(8,128)S(1)}, s32[16,512]{1,0:T(8,128)S(1)}, s32[16,512]{1,0:T(8,128)S(1)}, ...), condition=%wide.region_1.2_spmd.clone, body=%wide.region_0.1_spmd.clone.sunk | while | flops 806223872 | bytes 1067103 | solution.py:153
  21.2 34.9 %reshape_reshape.6 = f32[4,2,16,2,256,2]{5,4,3,2,1,0:T(8,128)} reshape(f32[256,512]{1,0:T(8,128)S(1)} %get-tuple-element.93) | data formatting | bytes 1048576 | tf_op jit(solution)/shard_map/reshape;reshape | solution.py:66
  56.1 11.6 %fusion.1208 = (f32[16,256]{1,0:T(8,128)S(1)}, f32[4,16,256]{2,1,0:T(8,128)S(1)}) fusion(f32[4,2,16,2,256,2]{5,4,3,2,1,0:T(8,128)} %reshape_reshape.6), kind=kLoop, calls=%fused_computation.2077 | loop fusion | flops 241664 | bytes 606208 | tf_op jit(solution)/shard_map/reduce_sum | solution.py:66
  67.7 5.5 %reshape.810 = f32[2,2,8,2,128,2]{5,4,3,2,1,0:T(8,128)} reshape(f32[4,16,256]{2,1,0:T(8,128)S(1)} %get-tuple-element.133) | data formatting | bytes 131072 | tf_op jit(solution)/shard_map/reshape | solution.py:66
  73.2 2.5 reduce_sum.100
  75.7 3.2 %collective-permute-start.12 = (f32[2,8,128]{2,1,0:T(8,128)S(1)}, f32[2,8,128]{2,1,0:T(8,128)S(1)}, u32[]{:S(2)}, u32[]{:S(2)}) collective-permute-start(f32[2,8,128]{2,1,0:T(8,128)S(1)} %reduce_sum.100), channel_id=1, source_target_pairs={{0,4},{4,8},{8,12},{12,16},{16,20},{20,24},{24,28},{1,5},{5,9},{9,... | collective-permute-start | bytes 24584 | tf_op jit(solution)/shard_map/ppermute | solution.py:25
  81.1 4.1 %collective-permute-start.4 = (f32[2,16,256]{2,0,1:T(2,128)S(1)}, f32[2,16,256]{2,0,1:T(2,128)S(1)}, u32[]{:S(2)}, u32[]{:S(2)}) collective-permute-start(f32[2,16,256]{2,0,1:T(2,128)S(1)} %get-tuple-element.190), channel_id=1, source_target_pairs={{0,4},{4,8},{8,12},{12,16},{16,20},{20,24},{24,28},{1,5},{5,9},{9,... | collective-permute-start | bytes 98312 | tf_op jit(solution)/shard_map/ppermute | solution.py:25
  87.1 4.3 %collective-permute-start = (f32[2,32,512]{2,1,0:T(8,128)S(1)}, f32[2,32,512]{2,1,0:T(8,128)S(1)}, u32[]{:S(2)}, u32[]{:S(2)}) collective-permute-start(f32[2,32,512]{2,1,0:T(8,128)S(1)} %bitcast.129), channel_id=1, source_target_pairs={{0,4},{4,8},{8,12},{12,16},{16,20},{20,24},{24,28},{1,5},{5,9},{9,... | collective-permute-start | bytes 393224 | tf_op jit(solution)/shard_map/ppermute | solution.py:25
  95.1 36.2 %all-gather = f32[32,1,336]{2,1,0:T(1,128)S(1)} all-gather(f32[1,1,336]{2,1,0:T(1,128)S(1)} %maximum_bitcast_fusion), channel_id=1, replica_groups=mesh['slab'=8,'pencil'=4] {'slab','pencil'}, dimensions={0}, use_global_device_ids=true | all-gather | bytes 44352 | tf_op jit(solution)/shard_map/all_gather | solution.py:192
  141.2 2.5 collective-permute-done.15
  146.0 5.2 %collective-permute-start.17 = (f32[1,8,128]{2,1,0:T(8,128)S(1)}, f32[1,8,128]{2,1,0:T(8,128)S(1)}, u32[]{:S(2)}, u32[]{:S(2)}) collective-permute-start(f32[1,8,128]{2,1,0:T(8,128)S(1)} %get-tuple-element.199), channel_id=1, source_target_pairs={{4,0},{8,4},{12,8},{16,12},{20,16},{24,20},{28,24},{5,1},{9,5},{13... | collective-permute-start | bytes 12296 | tf_op jit(solution)/shard_map/ppermute | solution.py:27
  157.7 3.5 %collective-permute-start.6 = (f32[8,2,256]{2,0,1:T(8,128)S(1)}, f32[8,2,256]{2,0,1:T(8,128)S(1)}, u32[]{:S(2)}, u32[]{:S(2)}) collective-permute-start(f32[8,2,256]{2,0,1:T(8,128)S(1)} %get-tuple-element.184), channel_id=1, source_target_pairs={{0,1},{1,2},{2,3},{4,5},{5,6},{6,7},{8,9},{9,10},{10,11},{12,13},{... | collective-permute-start | bytes 49160 | tf_op jit(solution)/shard_map/ppermute | solution.py:25
  163.2 3.1 %collective-permute-done.7 = f32[8,2,256]{2,0,1:T(8,128)S(1)} collective-permute-done((f32[8,2,256]{2,0,1:T(8,128)S(1)}, f32[8,2,256]{2,0,1:T(8,128)S(1)}, u32[]{:S(2)}, u32[]{:S(2)}) %collective-permute-start.7) | collective-permute-done | bytes 16416 | tf_op jit(solution)/shard_map/ppermute | solution.py:27
  166.6 2.7 %fusion.468 = f32[4,16,256]{2,0,1:T(4,128)S(1)} fusion(f32[8,20,260]{2,0,1:T(8,128)S(1)} %select_maximum_fusion.8, f32[8,18,256]{2,0,1:T(8,128)S(1)} %get-tuple-element.183, f32[2,16,256]{2,0,1:T(2,128)S(1)} %collective-permute-done.5, f32[4,16,256]{2,0,1:T(4,128)S(1)} %copy.47, f32[8,18,256]{2,0,1:T(8,128)S(1)} %get-tuple-element.182, ...), kind=kLoop, calls=%fused_computation.912 | loop fusion | flops 4145152 | bytes 8060928 | tf_op jit(solution)/shard_map/add | solution.py:53
  169.4 4.5 %collective-permute-start.8 = (f32[1,16,256]{2,0,1:T(1,128)S(1)}, f32[1,16,256]{2,0,1:T(1,128)S(1)}, u32[]{:S(2)}, u32[]{:S(2)}) collective-permute-start(f32[1,16,256]{2,0,1:T(1,128)S(1)} %get-tuple-element.188), channel_id=1, source_target_pairs={{0,4},{4,8},{8,12},{12,16},{16,20},{20,24},{24,28},{1,5},{5,9},{9,... | collective-permute-start | bytes 49160 | tf_op jit(solution)/shard_map/ppermute | solution.py:25
  176.1 3.2 %collective-permute-done.9 = f32[1,16,256]{2,0,1:T(1,128)S(1)} collective-permute-done((f32[1,16,256]{2,0,1:T(1,128)S(1)}, f32[1,16,256]{2,0,1:T(1,128)S(1)}, u32[]{:S(2)}, u32[]{:S(2)}) %collective-permute-start.9) | collective-permute-done | bytes 16416 | tf_op jit(solution)/shard_map/ppermute | solution.py:27
  179.3 3.4 %collective-permute-start.10 = (f32[6,1,256]{2,0,1:T(8,128)S(1)}, f32[6,1,256]{2,0,1:T(8,128)S(1)}, u32[]{:S(2)}, u32[]{:S(2)}) collective-permute-start(f32[6,1,256]{2,0,1:T(8,128)S(1)} %get-tuple-element.186), channel_id=1, source_target_pairs={{0,1},{1,2},{2,3},{4,5},{5,6},{6,7},{8,9},{9,10},{10,11},{12,13},{... | collective-permute-start | bytes 18440 | tf_op jit(solution)/shard_map/ppermute | solution.py:25
  184.9 2.7 %collective-permute-done.11 = f32[6,1,256]{2,0,1:T(8,128)S(1)} collective-permute-done((f32[6,1,256]{2,0,1:T(8,128)S(1)}, f32[6,1,256]{2,0,1:T(8,128)S(1)}, u32[]{:S(2)}, u32[]{:S(2)}) %collective-permute-start.11) | collective-permute-done | bytes 6176 | tf_op jit(solution)/shard_map/ppermute | solution.py:27
  192.9 2.6 collective-permute-done.3
  196.2 10.7 %convolution_add_fusion.5 = f32[8,32,512]{2,1,0:T(8,128)S(1)} fusion(f32[8,32,256]{2,1,0:T(8,128)S(1)} %convolution_bitcast_fusion, f32[12,36,516]{2,1,0:T(8,128)S(1)} %select_maximum_fusion.4, f32[12,34,512]{2,1,0:T(8,128)S(1)} %get-tuple-element.175, f32[2,32,512]{2,1,0:T(8,128)S(1)} %collective-permute-done.1, f32[8,32,512]{2,1,0:T(8,128)S(1)} %bitcast.118, ...), kind=kOutput, calls=%fused_computation.282 | convolution fusion | flops 436600832 | bytes 64495616 | tf_op jit(solution)/shard_map/fc,abc->abf/dot_general | solution.py:92
  212.3 4.3 %collective-permute-start.21 = (f32[2,32,512]{2,1,0:T(8,128)S(1)}, f32[2,32,512]{2,1,0:T(8,128)S(1)}, u32[]{:S(2)}, u32[]{:S(2)}) collective-permute-start(f32[2,32,512]{2,1,0:T(8,128)S(1)} %get-tuple-element.178), channel_id=1, source_target_pairs={{0,4},{4,8},{8,12},{12,16},{16,20},{20,24},{24,28},{1,5},{5,9},{9,... | collective-permute-start | bytes 393224 | tf_op jit(solution)/shard_map/ppermute | solution.py:25
  217.1 2.9 %collective-permute-done.21 = f32[2,32,512]{2,1,0:T(8,128)S(1)} collective-permute-done((f32[2,32,512]{2,1,0:T(8,128)S(1)}, f32[2,32,512]{2,1,0:T(8,128)S(1)}, u32[]{:S(2)}, u32[]{:S(2)}) %collective-permute-start.21) | collective-permute-done | bytes 131104 | tf_op jit(solution)/shard_map/ppermute | solution.py:25
  222.4 3.3 %collective-permute-start.23 = (f32[12,2,512]{2,1,0:T(2,128)S(1)}, f32[12,2,512]{2,1,0:T(2,128)S(1)}, u32[]{:S(2)}, u32[]{:S(2)}) collective-permute-start(f32[12,2,512]{2,1,0:T(2,128)S(1)} %get-tuple-element.172), channel_id=1, source_target_pairs={{0,1},{1,2},{2,3},{4,5},{5,6},{6,7},{8,9},{9,10},{10,11},{12,13},{... | collective-permute-start | bytes 147464 | tf_op jit(solution)/shard_map/ppermute | solution.py:25
  228.8 40.4 %while.26 = (s32[]{:T(128)}, f32[16,512,3]{1,2,0:T(4,128)}, f32[16,512]{1,0:T(8,128)S(1)}, s32[16,512]{1,0:T(8,128)S(1)}, f32[3,256,512]{1,2,0:T(8,128)S(1)}, /*index=5*/s32[16,512]{1,0:T(8,128)S(1)}, s32[]{:T(128)}) while((s32[]{:T(128)}, f32[16,512,3]{1,2,0:T(4,128)}, f32[16,512]{1,0:T(8,128)S(1)}, s32[16,512]{1,0:T(8,128)S(1)}, ...), condition=%wide.region_18.19_spmd.clone, body=%wide.region_16.18_spmd.clone.sunk | while | flops 2418147840 | bytes 3709525 | solution.py:252
  (278 shorter events, 109.8 us)
Async XLA Ops:
  75.7 61.1 %collective-permute-start.12 = (f32[2,8,128]{2,1,0:T(8,128)S(1)}, f32[2,8,128]{2,1,0:T(8,128)S(1)}, u32[]{:S(2)}, u32[]{:S(2)}) collective-permute-start(f32[2,8,128]{2,1,0:T(8,128)S(1)} %reduce_sum.100), channel_id=1, source_target_pairs={{0,4},{4,8},{8,12},{12,16},{16,20},{20,24},{24,28},{1,5},{5,9},{9,... | collective-permute-start | bytes 24584 | tf_op jit(solution)/shard_map/ppermute | solution.py:25
  78.9 57.9 %collective-permute-start.13 = (f32[2,8,128]{2,1,0:T(8,128)S(1)}, f32[2,8,128]{2,1,0:T(8,128)S(1)}, u32[]{:S(2)}, u32[]{:S(2)}) collective-permute-start(f32[2,8,128]{2,1,0:T(8,128)S(1)} %reduce_sum.100), channel_id=1, source_target_pairs={{4,0},{8,4},{12,8},{16,12},{20,16},{24,20},{28,24},{5,1},{9,5},{13... | collective-permute-start | bytes 24584 | tf_op jit(solution)/shard_map/ppermute | solution.py:27
  81.1 74.5 %collective-permute-start.4 = (f32[2,16,256]{2,0,1:T(2,128)S(1)}, f32[2,16,256]{2,0,1:T(2,128)S(1)}, u32[]{:S(2)}, u32[]{:S(2)}) collective-permute-start(f32[2,16,256]{2,0,1:T(2,128)S(1)} %get-tuple-element.190), channel_id=1, source_target_pairs={{0,4},{4,8},{8,12},{12,16},{16,20},{20,24},{24,28},{1,5},{5,9},{9,... | collective-permute-start | bytes 98312 | tf_op jit(solution)/shard_map/ppermute | solution.py:25
  85.2 72.5 %collective-permute-start.5 = (f32[2,16,256]{2,0,1:T(2,128)S(1)}, f32[2,16,256]{2,0,1:T(2,128)S(1)}, u32[]{:S(2)}, u32[]{:S(2)}) collective-permute-start(f32[2,16,256]{2,0,1:T(2,128)S(1)} %get-tuple-element.191), channel_id=1, source_target_pairs={{4,0},{8,4},{12,8},{16,12},{20,16},{24,20},{28,24},{5,1},{9,5},{13... | collective-permute-start | bytes 98312 | tf_op jit(solution)/shard_map/ppermute | solution.py:27
  87.1 100.9 %collective-permute-start = (f32[2,32,512]{2,1,0:T(8,128)S(1)}, f32[2,32,512]{2,1,0:T(8,128)S(1)}, u32[]{:S(2)}, u32[]{:S(2)}) collective-permute-start(f32[2,32,512]{2,1,0:T(8,128)S(1)} %bitcast.129), channel_id=1, source_target_pairs={{0,4},{4,8},{8,12},{12,16},{16,20},{20,24},{24,28},{1,5},{5,9},{9,... | collective-permute-start | bytes 393224 | tf_op jit(solution)/shard_map/ppermute | solution.py:25
  136.8 4.4 %collective-permute-start.14 = (f32[6,2,128]{2,1,0:T(2,128)S(1)}, f32[6,2,128]{2,1,0:T(2,128)S(1)}, u32[]{:S(2)}, u32[]{:S(2)}) collective-permute-start(f32[6,2,128]{2,1,0:T(2,128)S(1)} %get-tuple-element.194), channel_id=1, source_target_pairs={{0,1},{1,2},{2,3},{4,5},{5,6},{6,7},{8,9},{9,10},{10,11},{12,13},{... | collective-permute-start | bytes 18440 | tf_op jit(solution)/shard_map/ppermute | solution.py:25
  138.8 4.9 %collective-permute-start.15 = (f32[6,2,128]{2,1,0:T(2,128)S(1)}, f32[6,2,128]{2,1,0:T(2,128)S(1)}, u32[]{:S(2)}, u32[]{:S(2)}) collective-permute-start(f32[6,2,128]{2,1,0:T(2,128)S(1)} %get-tuple-element.195), channel_id=1, source_target_pairs={{1,0},{2,1},{3,2},{5,4},{6,5},{7,6},{9,8},{10,9},{11,10},{13,12},{... | collective-permute-start | bytes 18440 | tf_op jit(solution)/shard_map/ppermute | solution.py:27
  144.1 7.1 %collective-permute-start.16 = (f32[1,8,128]{2,1,0:T(8,128)S(1)}, f32[1,8,128]{2,1,0:T(8,128)S(1)}, u32[]{:S(2)}, u32[]{:S(2)}) collective-permute-start(f32[1,8,128]{2,1,0:T(8,128)S(1)} %get-tuple-element.198), channel_id=1, source_target_pairs={{0,4},{4,8},{8,12},{12,16},{16,20},{20,24},{24,28},{1,5},{5,9},{9,... | collective-permute-start | bytes 12296 | tf_op jit(solution)/shard_map/ppermute | solution.py:25
  146.0 7.1 %collective-permute-start.17 = (f32[1,8,128]{2,1,0:T(8,128)S(1)}, f32[1,8,128]{2,1,0:T(8,128)S(1)}, u32[]{:S(2)}, u32[]{:S(2)}) collective-permute-start(f32[1,8,128]{2,1,0:T(8,128)S(1)} %get-tuple-element.199), channel_id=1, source_target_pairs={{4,0},{8,4},{12,8},{16,12},{20,16},{24,20},{28,24},{5,1},{9,5},{13... | collective-permute-start | bytes 12296 | tf_op jit(solution)/shard_map/ppermute | solution.py:27
  151.2 36.8 %collective-permute-start.1 = (f32[2,32,512]{2,1,0:T(8,128)S(1)}, f32[2,32,512]{2,1,0:T(8,128)S(1)}, u32[]{:S(2)}, u32[]{:S(2)}) collective-permute-start(f32[2,32,512]{2,1,0:T(8,128)S(1)} %bitcast.128), channel_id=1, source_target_pairs={{4,0},{8,4},{12,8},{16,12},{20,16},{24,20},{28,24},{5,1},{9,5},{13... | collective-permute-start | bytes 393224 | tf_op jit(solution)/shard_map/ppermute | solution.py:27
  153.2 8.0 %collective-permute-start.18 = (f32[4,1,128]{2,1,0:T(1,128)S(1)}, f32[4,1,128]{2,1,0:T(1,128)S(1)}, u32[]{:S(2)}, u32[]{:S(2)}) collective-permute-start(f32[4,1,128]{2,1,0:T(1,128)S(1)} %get-tuple-element.196), channel_id=1, source_target_pairs={{0,1},{1,2},{2,3},{4,5},{5,6},{6,7},{8,9},{9,10},{10,11},{12,13},{... | collective-permute-start | bytes 6152 | tf_op jit(solution)/shard_map/ppermute | solution.py:25
  155.6 7.6 %collective-permute-start.19 = (f32[4,1,128]{2,1,0:T(1,128)S(1)}, f32[4,1,128]{2,1,0:T(1,128)S(1)}, u32[]{:S(2)}, u32[]{:S(2)}) collective-permute-start(f32[4,1,128]{2,1,0:T(1,128)S(1)} %get-tuple-element.197), channel_id=1, source_target_pairs={{1,0},{2,1},{3,2},{5,4},{6,5},{7,6},{9,8},{10,9},{11,10},{13,12},{... | collective-permute-start | bytes 6152 | tf_op jit(solution)/shard_map/ppermute | solution.py:27
  157.7 5.4 %collective-permute-start.6 = (f32[8,2,256]{2,0,1:T(8,128)S(1)}, f32[8,2,256]{2,0,1:T(8,128)S(1)}, u32[]{:S(2)}, u32[]{:S(2)}) collective-permute-start(f32[8,2,256]{2,0,1:T(8,128)S(1)} %get-tuple-element.184), channel_id=1, source_target_pairs={{0,1},{1,2},{2,3},{4,5},{5,6},{6,7},{8,9},{9,10},{10,11},{12,13},{... | collective-permute-start | bytes 49160 | tf_op jit(solution)/shard_map/ppermute | solution.py:25
  161.2 5.1 %collective-permute-start.7 = (f32[8,2,256]{2,0,1:T(8,128)S(1)}, f32[8,2,256]{2,0,1:T(8,128)S(1)}, u32[]{:S(2)}, u32[]{:S(2)}) collective-permute-start(f32[8,2,256]{2,0,1:T(8,128)S(1)} %get-tuple-element.185), channel_id=1, source_target_pairs={{1,0},{2,1},{3,2},{5,4},{6,5},{7,6},{9,8},{10,9},{11,10},{13,12},{... | collective-permute-start | bytes 49160 | tf_op jit(solution)/shard_map/ppermute | solution.py:27
  169.4 6.7 %collective-permute-start.8 = (f32[1,16,256]{2,0,1:T(1,128)S(1)}, f32[1,16,256]{2,0,1:T(1,128)S(1)}, u32[]{:S(2)}, u32[]{:S(2)}) collective-permute-start(f32[1,16,256]{2,0,1:T(1,128)S(1)} %get-tuple-element.188), channel_id=1, source_target_pairs={{0,4},{4,8},{8,12},{12,16},{16,20},{20,24},{24,28},{1,5},{5,9},{9,... | collective-permute-start | bytes 49160 | tf_op jit(solution)/shard_map/ppermute | solution.py:25
  173.9 5.4 %collective-permute-start.9 = (f32[1,16,256]{2,0,1:T(1,128)S(1)}, f32[1,16,256]{2,0,1:T(1,128)S(1)}, u32[]{:S(2)}, u32[]{:S(2)}) collective-permute-start(f32[1,16,256]{2,0,1:T(1,128)S(1)} %get-tuple-element.189), channel_id=1, source_target_pairs={{4,0},{8,4},{12,8},{16,12},{20,16},{24,20},{28,24},{5,1},{9,5},{13... | collective-permute-start | bytes 49160 | tf_op jit(solution)/shard_map/ppermute | solution.py:27
  179.3 5.6 %collective-permute-start.10 = (f32[6,1,256]{2,0,1:T(8,128)S(1)}, f32[6,1,256]{2,0,1:T(8,128)S(1)}, u32[]{:S(2)}, u32[]{:S(2)}) collective-permute-start(f32[6,1,256]{2,0,1:T(8,128)S(1)} %get-tuple-element.186), channel_id=1, source_target_pairs={{0,1},{1,2},{2,3},{4,5},{5,6},{6,7},{8,9},{9,10},{10,11},{12,13},{... | collective-permute-start | bytes 18440 | tf_op jit(solution)/shard_map/ppermute | solution.py:25
  182.7 5.0 %collective-permute-start.11 = (f32[6,1,256]{2,0,1:T(8,128)S(1)}, f32[6,1,256]{2,0,1:T(8,128)S(1)}, u32[]{:S(2)}, u32[]{:S(2)}) collective-permute-start(f32[6,1,256]{2,0,1:T(8,128)S(1)} %get-tuple-element.187), channel_id=1, source_target_pairs={{1,0},{2,1},{3,2},{5,4},{6,5},{7,6},{9,8},{10,9},{11,10},{13,12},{... | collective-permute-start | bytes 18440 | tf_op jit(solution)/shard_map/ppermute | solution.py:27
  188.1 4.8 %collective-permute-start.2 = (f32[12,2,512]{2,1,0:T(2,128)S(1)}, f32[12,2,512]{2,1,0:T(2,128)S(1)}, u32[]{:S(2)}, u32[]{:S(2)}) collective-permute-start(f32[12,2,512]{2,1,0:T(2,128)S(1)} %get-tuple-element.176), channel_id=1, source_target_pairs={{0,1},{1,2},{2,3},{4,5},{5,6},{6,7},{8,9},{9,10},{10,11},{12,13},{... | collective-permute-start | bytes 147464 | tf_op jit(solution)/shard_map/ppermute | solution.py:25
  190.0 5.4 %collective-permute-start.3 = (f32[12,2,512]{2,1,0:T(2,128)S(1)}, f32[12,2,512]{2,1,0:T(2,128)S(1)}, u32[]{:S(2)}, u32[]{:S(2)}) collective-permute-start(f32[12,2,512]{2,1,0:T(2,128)S(1)} %get-tuple-element.177), channel_id=1, source_target_pairs={{1,0},{2,1},{3,2},{5,4},{6,5},{7,6},{9,8},{10,9},{11,10},{13,12},{... | collective-permute-start | bytes 147464 | tf_op jit(solution)/shard_map/ppermute | solution.py:27
  210.3 6.8 %collective-permute-start.20 = (f32[2,32,512]{2,1,0:T(8,128)S(1)}, f32[2,32,512]{2,1,0:T(8,128)S(1)}, u32[]{:S(2)}, u32[]{:S(2)}) collective-permute-start(f32[2,32,512]{2,1,0:T(8,128)S(1)} %get-tuple-element.179), channel_id=1, source_target_pairs={{4,0},{8,4},{12,8},{16,12},{20,16},{24,20},{28,24},{5,1},{9,5},{13... | collective-permute-start | bytes 393224 | tf_op jit(solution)/shard_map/ppermute | solution.py:27
  212.3 7.7 %collective-permute-start.21 = (f32[2,32,512]{2,1,0:T(8,128)S(1)}, f32[2,32,512]{2,1,0:T(8,128)S(1)}, u32[]{:S(2)}, u32[]{:S(2)}) collective-permute-start(f32[2,32,512]{2,1,0:T(8,128)S(1)} %get-tuple-element.178), channel_id=1, source_target_pairs={{0,4},{4,8},{8,12},{12,16},{16,20},{20,24},{24,28},{1,5},{5,9},{9,... | collective-permute-start | bytes 393224 | tf_op jit(solution)/shard_map/ppermute | solution.py:25
  220.0 5.9 %collective-permute-start.22 = (f32[12,2,512]{2,1,0:T(2,128)S(1)}, f32[12,2,512]{2,1,0:T(2,128)S(1)}, u32[]{:S(2)}, u32[]{:S(2)}) collective-permute-start(f32[12,2,512]{2,1,0:T(2,128)S(1)} %get-tuple-element.173), channel_id=1, source_target_pairs={{1,0},{2,1},{3,2},{5,4},{6,5},{7,6},{9,8},{10,9},{11,10},{13,12},{... | collective-permute-start | bytes 147464 | tf_op jit(solution)/shard_map/ppermute | solution.py:27
  222.4 4.4 %collective-permute-start.23 = (f32[12,2,512]{2,1,0:T(2,128)S(1)}, f32[12,2,512]{2,1,0:T(2,128)S(1)}, u32[]{:S(2)}, u32[]{:S(2)}) collective-permute-start(f32[12,2,512]{2,1,0:T(2,128)S(1)} %get-tuple-element.172), channel_id=1, source_target_pairs={{0,1},{1,2},{2,3},{4,5},{5,6},{6,7},{8,9},{9,10},{10,11},{12,13},{... | collective-permute-start | bytes 147464 | tf_op jit(solution)/shard_map/ppermute | solution.py:25
  (1 other events, 17.1 us)
where the time goes:
time: 271 us; the launch traced here: 269 us
  starting transfers between devices  66.6 us (25%)
  matrix products  65.5 us (24%)
  local copies, waits for them, and re-layouts  44.9 us (17%)
  blocking collectives  36.2 us (13%)
  other arithmetic  35 us (13%)
  waiting for transfers between devices  18.4 us (7%)
    ppermute x12, starting transfers between devices, extended(): lax.ppermute(tail, axis, [(i, (i + 1) % count) for i in range(ends)])  38.6 us
    all_gather x1, blocking collectives, body(): gathered = lax.all_gather(packed, ('slab', 'pencil'), axis=0, tiled=True)  36.2 us
    another operation x1, local copies, waits for them, and re-layouts, restrict(): grid.reshape(planes // 2, 2, rows // 2, 2, length // 2, 2)  34.9 us
    ppermute x12, starting transfers between devices, extended(): lax.ppermute(head, axis, [((i + 1) % count, i) for i in range(ends)])  28 us
    dot_general x16, matrix products, pick(): jnp.einsum('ar,drx->adx', row_table, gradients, precision=lax.Precision.H...  27.9 us
    dot_general x16, matrix products, deposit(): added = jnp.dot(row_table.T, column_table, precision=lax.Precision.HIGHEST)  17.5 us
    ppermute x12, waiting for transfers between devices, extended(): lax.ppermute(head, axis, [((i + 1) % count, i) for i in range(ends)])  14.7 us
    reduce_sum x4, other arithmetic, restrict(): grid.reshape(planes // 2, 2, rows // 2, 2, length // 2, 2)  14.4 us
  transfers between devices with their start and end apart: 24, of which 8 were waited for; matrix products, arithmetic and copies ran while one was open for 5% of the time, Pallas kernels for 0%

commit v1 on v0

--- a/solution.py
+++ b/solution.py
@@ -4,6 +4,8 @@
 import jax
 import jax.numpy as jnp
 from jax import lax
+from jax.experimental import pallas as pl
+from jax.experimental.pallas import tpu as pltpu
 from jax.sharding import PartitionSpec as P
 
 CZ = 8
@@ -124,35 +126,103 @@
     return (8.0 * (shifted(1) - shifted(-1)) - (shifted(2) - shifted(-2))) / 12.0
 
 
+CHUNK = 1024
+
+
+def split_two(values):
+    high = values.astype(jnp.bfloat16)
+    return high, (values - high.astype(jnp.float32)).astype(jnp.bfloat16)
+
+
+def local_rows(cell_ref, start, width):
+    z0 = lax.axis_index("slab") * CZ
+    y0 = lax.axis_index("pencil") * CY
+    plane = cell_ref[0:1, pl.ds(start, width)] - z0
+    line = cell_ref[1:2, pl.ds(start, width)] - y0
+    return plane * CY + line, cell_ref[2:3, pl.ds(start, width)]
+
+
+def deposit_kernel(cell_ref, charge_ref, grid_ref):
+    atoms = cell_ref.shape[1]
+    width = math.gcd(atoms, CHUNK)
+    rows_total = CZ * CY
+    grid_ref[...] = jnp.zeros_like(grid_ref)
+
+    @pl.loop(0, atoms // width)
+    def _(step):
+        start = pl.multiple_of(step * width, width)
+        rows, columns = local_rows(cell_ref, start, width)
+        charges = charge_ref[:, pl.ds(start, width)]
+        high = charges.astype(jnp.bfloat16).astype(jnp.float32)
+        low = charges - high
+        at_row = lax.broadcasted_iota(jnp.int32, (rows_total, width), 0) == rows
+        at_column = lax.broadcasted_iota(jnp.int32, (NX, width), 0) == columns
+        table = jnp.where(at_column, 1.0, 0.0).astype(jnp.bfloat16)
+        stacked = jnp.concatenate(
+            [
+                jnp.where(at_row, high, 0.0).astype(jnp.bfloat16),
+                jnp.where(at_row, low, 0.0).astype(jnp.bfloat16),
+            ],
+            axis=0,
+        )
+        added = lax.dot_general(
+            stacked, table, (((1,), (1,)), ((), ())), preferred_element_type=jnp.float32
+        )
+        grid_ref[...] += added[:rows_total] + added[rows_total:]
+
+
+def deposit_call(atom_cell, charge):
+    return pl.pallas_call(
+        deposit_kernel,
+        out_shape=jax.ShapeDtypeStruct((CZ * CY, NX), jnp.float32),
+        compiler_params=pltpu.CompilerParams(vmem_limit_bytes=48 * 2**20),
+    )(atom_cell, charge.reshape(1, -1))
+
+
+def pick_forces(cell_ref, charge_ref, high_ref, low_ref, force_ref):
+    atoms = cell_ref.shape[1]
+    width = math.gcd(atoms, 512)
+    rows_total = CZ * CY
+
+    @pl.loop(0, atoms // width)
+    def _(step):
+        start = pl.multiple_of(step * width, width)
+        rows, columns = local_rows(cell_ref, start, width)
+        charges = charge_ref[:, pl.ds(start, width)]
+        at_row = lax.broadcasted_iota(jnp.int32, (rows_total, width), 0) == rows
+        at_column = lax.broadcasted_iota(jnp.int32, (NX, width), 0) == columns
+        table = jnp.where(at_column, 1.0, 0.0).astype(jnp.bfloat16)
+        for direction in range(3):
+            part = pl.ds(direction * rows_total, rows_total)
+            at_cell = jnp.dot(high_ref[part, :], table, preferred_element_type=jnp.float32)
+            at_cell += jnp.dot(low_ref[part, :], table, preferred_element_type=jnp.float32)
+            chosen = jnp.sum(jnp.where(at_row, at_cell, 0.0), axis=0, keepdims=True)
+            force_ref[direction : direction + 1, pl.ds(start, width)] = -charges * chosen
+
+
+def pick_kernel(cell_ref, charge_ref, grad_ref, force_ref, high_ref, low_ref):
+    high, low = split_two(grad_ref[...])
+    high_ref[...] = high
+    low_ref[...] = low
+    pick_forces(cell_ref, charge_ref, high_ref, low_ref, force_ref)
+
+
+def pick_call(atom_cell, charge, gradients):
+    rows = gradients.shape[0]
+    return pl.pallas_call(
+        pick_kernel,
+        out_shape=jax.ShapeDtypeStruct(atom_cell.shape, jnp.float32),
+        scratch_shapes=[pltpu.VMEM((rows, NX), jnp.bfloat16)] * 2,
+        compiler_params=pltpu.CompilerParams(vmem_limit_bytes=48 * 2**20),
+    )(atom_cell, charge.reshape(1, -1), gradients)
+
+
 def body(atom_cell, charge):
     slab_pos = lax.axis_index("slab")
     pencil_pos = lax.axis_index("pencil")
     slabs = lax.axis_size("slab")
     pencils = lax.axis_size("pencil")
-    atom_total = charge.shape[0]
-    row_cells = CZ * CY
-    plane_row = (atom_cell[0] - slab_pos * CZ) * CY + (atom_cell[1] - pencil_pos * CY)
-    column_of = atom_cell[2]
-    block_atoms = math.gcd(atom_total, 512)
-    block_count = atom_total // block_atoms
-    row_blocks = plane_row.reshape(block_count, block_atoms)
-    column_blocks = column_of.reshape(block_count, block_atoms)
-    charge_blocks = charge.reshape(block_count, block_atoms)
-    row_range = jnp.arange(row_cells, dtype=jnp.int32)
-    column_range = jnp.arange(NX, dtype=jnp.int32)
-
-    def deposit(total, block):
-        rows_here, columns_here, charges_here = block
-        row_table = (rows_here[:, None] == row_range[None, :]).astype(jnp.float32)
-        column_table = jnp.where(
-            columns_here[:, None] == column_range[None, :], charges_here[:, None], 0.0
-        )
-        added = jnp.dot(row_table.T, column_table, precision=lax.Precision.HIGHEST)
-        return (total + added, None)
-
-    charge_grid, _ = lax.scan(
-        deposit, jnp.zeros((row_cells, NX), jnp.float32), (row_blocks, column_blocks, charge_blocks)
-    )
+    charge_grid = deposit_call(atom_cell, charge)
     charge_grid = charge_grid.reshape(CZ, CY, NX)
     plane_ids = slab_pos * CZ + jnp.arange(CZ, dtype=jnp.int32)
     line_ids = pencil_pos * CY + jnp.arange(CY, dtype=jnp.int32)
@@ -237,20 +307,8 @@
     padded_field = jnp.pad(rimmed_field, ((0, 0), (0, 0), (2, 2)))
     gradients = jnp.stack(
         [gradient_along(padded_field, direction, CZ, CY, NX) for direction in range(3)]
-    ).reshape(3, row_cells, NX)
-
-    def pick(block):
-        rows_here, columns_here, charges_here = block
-        row_table = (rows_here[:, None] == row_range[None, :]).astype(jnp.float32)
-        column_table = (columns_here[:, None] == column_range[None, :]).astype(jnp.float32)
-        picked_rows = jnp.einsum(
-            "ar,drx->adx", row_table, gradients, precision=lax.Precision.HIGHEST
-        )
-        at_cell = jnp.sum(picked_rows * column_table[:, None, :], axis=2)
-        return -charges_here[:, None] * at_cell
-
-    picked = lax.map(pick, (row_blocks, column_blocks, charge_blocks))
-    forces = picked.reshape(atom_total, 3).T
+    ).reshape(3 * CZ * CY, NX)
+    forces = pick_call(atom_cell, charge, gradients)
     return (potential, forces)
 
 

time: 271 us -> 235 us (0.87)
  matrix products: 65.5 us -> 20 us
  Pallas kernels: 0 us -> 23.7 us
  other arithmetic: 35 us -> 21.8 us
    dot_general x32 -> x0, matrix products: 45.4 us -> none  [the longest x16 27.9 us: pick(): jnp.einsum('ar,drx->adx', row_table, gradients, precision=lax.Precision.H...]
    pallas_call x0 -> x2, Pallas kernels: none -> 23.7 us  [the longest x1 17.7 us: pick_call(): pl.pallas_call(pick_kernel, out_shape=jax.ShapeDtypeStruct(atom_cell.shap...]
    dynamic_update_slice x16 -> x0, other arithmetic: 9.73 us -> none  [body(): picked = lax.map(pick, (row_blocks, column_blocks, charge_blocks))]
  transfers between devices with their start and end apart: 24 -> 24, of which waited for: 8 -> 8; matrix products, arithmetic and copies ran while one was open for 5% -> 6% of each run, Pallas kernels for 0% -> 0%
where the time goes in v1:
time: 235 us; the launch traced here: 234 us
  starting transfers between devices  66.6 us (28%)
  local copies, waits for them, and re-layouts  45.4 us (19%)
  blocking collectives  36.2 us (15%)
  Pallas kernels  23.7 us (10%)
  other arithmetic  21.8 us (9%)
  matrix products  20 us (9%)
  waiting for transfers between devices  18.5 us (8%)
    ppermute x12, starting transfers between devices, extended(): lax.ppermute(tail, axis, [(i, (i + 1) % count) for i in range(ends)])  38.4 us
    all_gather x1, blocking collectives, body(): gathered = lax.all_gather(packed, ('slab', 'pencil'), axis=0, tiled=True)  36.2 us
    another operation x1, local copies, waits for them, and re-layouts, restrict(): grid.reshape(planes // 2, 2, rows // 2, 2, length // 2, 2)  34.9 us
    ppermute x12, starting transfers between devices, extended(): lax.ppermute(head, axis, [((i + 1) % count, i) for i in range(ends)])  28.1 us
    pallas_call x1, Pallas kernels, pick_call(): pl.pallas_call(pick_kernel, out_shape=jax.ShapeDtypeStruct(atom_cell.shap...  17.7 us
    ppermute x12, waiting for transfers between devices, extended(): lax.ppermute(head, axis, [((i + 1) % count, i) for i in range(ends)])  14.5 us
    reduce_sum x4, other arithmetic, restrict(): grid.reshape(planes // 2, 2, rows // 2, 2, length // 2, 2)  14.4 us
    dot_general x5, matrix products, to_fine(): jnp.einsum('fc,abc->abf', along_x, section, precision=lax.Precision.HIGHEST)  14 us
  transfers between devices with their start and end apart: 24, of which 8 were waited for; matrix products, arithmetic and copies ran while one was open for 6% of the time, Pallas kernels for 0%

profile of v1, /device:TPU:3, one launch (start us, length us, event | category | flops | bytes accessed | tf_op | source)
XLA Modules:
  0.0 233.8 jit_solution(14471167684279762392)
XLA Ops:
  2.3 6.0 %shard_map.41 = f32[256,512]{1,0:T(8,128)S(1)} custom-call(s32[3,8192]{1,0:T(4,128)S(1)} %copy-done, f32[1,8192]{1,0:T(1,128)S(1)} %bitcast.90), custom_call_target="tpu_custom_call" | custom-call | tf_op jit(solution)/shard_map/pallas_call | solution.py:175
  8.3 34.9 %reshape_reshape.6 = f32[4,2,16,2,256,2]{5,4,3,2,1,0:T(8,128)} reshape(f32[256,512]{1,0:T(8,128)S(1)} %shard_map.41) | data formatting | bytes 1048576 | tf_op jit(solution)/shard_map/reshape;reshape | solution.py:68
  43.2 11.6 %fusion.1192 = (f32[16,256]{1,0:T(8,128)S(1)}, f32[4,16,256]{2,1,0:T(8,128)S(1)}) fusion(f32[4,2,16,2,256,2]{5,4,3,2,1,0:T(8,128)} %reshape_reshape.6), kind=kLoop, calls=%fused_computation.2051 | loop fusion | flops 241664 | bytes 606208 | tf_op jit(solution)/shard_map/reduce_sum | solution.py:68
  54.7 5.5 %reshape.720 = f32[2,2,8,2,128,2]{5,4,3,2,1,0:T(8,128)} reshape(f32[4,16,256]{2,1,0:T(8,128)S(1)} %get-tuple-element.11) | data formatting | bytes 131072 | tf_op jit(solution)/shard_map/reshape | solution.py:68
  60.3 2.5 %reduce_sum.91 = f32[2,8,128]{2,1,0:T(8,128)S(1)} reduce(f32[2,2,8,2,128,2]{5,4,3,2,1,0:T(8,128)} %reshape.720, f32[]{:T(128)} %constant.419.clone.1), dimensions={1,3,5}, to_apply=%region_1.2 | reduce | flops 14336 | bytes 73732 | tf_op jit(solution)/shard_map/reduce_sum | solution.py:68
  62.8 3.2 %collective-permute-start.12 = (f32[2,8,128]{2,1,0:T(8,128)S(1)}, f32[2,8,128]{2,1,0:T(8,128)S(1)}, u32[]{:S(2)}, u32[]{:S(2)}) collective-permute-start(f32[2,8,128]{2,1,0:T(8,128)S(1)} %reduce_sum.91), channel_id=1, source_target_pairs={{0,4},{4,8},{8,12},{12,16},{16,20},{20,24},{24,28},{1,5},{5,9},{9,... | collective-permute-start | bytes 24584 | tf_op jit(solution)/shard_map/ppermute | solution.py:27
  68.2 4.1 %collective-permute-start.4 = (f32[2,16,256]{2,0,1:T(2,128)S(1)}, f32[2,16,256]{2,0,1:T(2,128)S(1)}, u32[]{:S(2)}, u32[]{:S(2)}) collective-permute-start(f32[2,16,256]{2,0,1:T(2,128)S(1)} %get-tuple-element.44), channel_id=1, source_target_pairs={{0,4},{4,8},{8,12},{12,16},{16,20},{20,24},{24,28},{1,5},{5,9},{9,... | collective-permute-start | bytes 98312 | tf_op jit(solution)/shard_map/ppermute | solution.py:27
  74.2 4.3 %collective-permute-start = (f32[2,32,512]{2,1,0:T(8,128)S(1)}, f32[2,32,512]{2,1,0:T(8,128)S(1)}, u32[]{:S(2)}, u32[]{:S(2)}) collective-permute-start(f32[2,32,512]{2,1,0:T(8,128)S(1)} %bitcast.96), channel_id=1, source_target_pairs={{0,4},{4,8},{8,12},{12,16},{16,20},{20,24},{24,28},{1,5},{5,9},{9,... | collective-permute-start | bytes 393224 | tf_op jit(solution)/shard_map/ppermute | solution.py:27
  82.2 36.2 %all-gather = f32[32,1,336]{2,1,0:T(1,128)S(1)} all-gather(f32[1,1,336]{2,1,0:T(1,128)S(1)} %maximum_bitcast_fusion), channel_id=1, replica_groups=mesh['slab'=8,'pencil'=4] {'slab','pencil'}, dimensions={0}, use_global_device_ids=true | all-gather | bytes 44352 | tf_op jit(solution)/shard_map/all_gather | solution.py:262
  128.3 2.5 %collective-permute-done.15 = f32[6,2,128]{2,1,0:T(2,128)S(1)} collective-permute-done((f32[6,2,128]{2,1,0:T(2,128)S(1)}, f32[6,2,128]{2,1,0:T(2,128)S(1)}, u32[]{:S(2)}, u32[]{:S(2)}) %collective-permute-start.15) | collective-permute-done | bytes 6176 | tf_op jit(solution)/shard_map/ppermute | solution.py:29
  133.1 5.2 %collective-permute-start.17 = (f32[1,8,128]{2,1,0:T(8,128)S(1)}, f32[1,8,128]{2,1,0:T(8,128)S(1)}, u32[]{:S(2)}, u32[]{:S(2)}) collective-permute-start(f32[1,8,128]{2,1,0:T(8,128)S(1)} %get-tuple-element.53), channel_id=1, source_target_pairs={{4,0},{8,4},{12,8},{16,12},{20,16},{24,20},{28,24},{5,1},{9,5},{13... | collective-permute-start | bytes 12296 | tf_op jit(solution)/shard_map/ppermute | solution.py:29
  144.7 3.5 %collective-permute-start.6 = (f32[8,2,256]{2,0,1:T(8,128)S(1)}, f32[8,2,256]{2,0,1:T(8,128)S(1)}, u32[]{:S(2)}, u32[]{:S(2)}) collective-permute-start(f32[8,2,256]{2,0,1:T(8,128)S(1)} %get-tuple-element.38), channel_id=1, source_target_pairs={{0,1},{1,2},{2,3},{4,5},{5,6},{6,7},{8,9},{9,10},{10,11},{12,13},{... | collective-permute-start | bytes 49160 | tf_op jit(solution)/shard_map/ppermute | solution.py:27
  150.3 2.9 %collective-permute-done.7 = f32[8,2,256]{2,0,1:T(8,128)S(1)} collective-permute-done((f32[8,2,256]{2,0,1:T(8,128)S(1)}, f32[8,2,256]{2,0,1:T(8,128)S(1)}, u32[]{:S(2)}, u32[]{:S(2)}) %collective-permute-start.7) | collective-permute-done | bytes 16416 | tf_op jit(solution)/shard_map/ppermute | solution.py:29
  153.5 2.7 %fusion.452 = f32[4,16,256]{2,0,1:T(4,128)S(1)} fusion(f32[8,20,260]{2,0,1:T(8,128)S(1)} %select_maximum_fusion.8, f32[8,18,256]{2,0,1:T(8,128)S(1)} %get-tuple-element.37, f32[2,16,256]{2,0,1:T(2,128)S(1)} %collective-permute-done.5, f32[4,16,256]{2,0,1:T(4,128)S(1)} %copy.35, f32[8,18,256]{2,0,1:T(8,128)S(1)} %get-tuple-element.36, ...), kind=kLoop, calls=%fused_computation.888 | loop fusion | flops 4145152 | bytes 8060928 | tf_op jit(solution)/shard_map/add | solution.py:55
  156.3 4.5 %collective-permute-start.8 = (f32[1,16,256]{2,0,1:T(1,128)S(1)}, f32[1,16,256]{2,0,1:T(1,128)S(1)}, u32[]{:S(2)}, u32[]{:S(2)}) collective-permute-start(f32[1,16,256]{2,0,1:T(1,128)S(1)} %get-tuple-element.42), channel_id=1, source_target_pairs={{0,4},{4,8},{8,12},{12,16},{16,20},{20,24},{24,28},{1,5},{5,9},{9,... | collective-permute-start | bytes 49160 | tf_op jit(solution)/shard_map/ppermute | solution.py:27
  163.0 3.2 %collective-permute-done.9 = f32[1,16,256]{2,0,1:T(1,128)S(1)} collective-permute-done((f32[1,16,256]{2,0,1:T(1,128)S(1)}, f32[1,16,256]{2,0,1:T(1,128)S(1)}, u32[]{:S(2)}, u32[]{:S(2)}) %collective-permute-start.9) | collective-permute-done | bytes 16416 | tf_op jit(solution)/shard_map/ppermute | solution.py:29
  166.3 3.4 %collective-permute-start.10 = (f32[6,1,256]{2,0,1:T(8,128)S(1)}, f32[6,1,256]{2,0,1:T(8,128)S(1)}, u32[]{:S(2)}, u32[]{:S(2)}) collective-permute-start(f32[6,1,256]{2,0,1:T(8,128)S(1)} %get-tuple-element.40), channel_id=1, source_target_pairs={{0,1},{1,2},{2,3},{4,5},{5,6},{6,7},{8,9},{9,10},{10,11},{12,13},{... | collective-permute-start | bytes 18440 | tf_op jit(solution)/shard_map/ppermute | solution.py:27
  171.9 2.7 %collective-permute-done.11 = f32[6,1,256]{2,0,1:T(8,128)S(1)} collective-permute-done((f32[6,1,256]{2,0,1:T(8,128)S(1)}, f32[6,1,256]{2,0,1:T(8,128)S(1)}, u32[]{:S(2)}, u32[]{:S(2)}) %collective-permute-start.11) | collective-permute-done | bytes 6176 | tf_op jit(solution)/shard_map/ppermute | solution.py:29
  179.8 2.6 %collective-permute-done.3 = f32[12,2,512]{2,1,0:T(2,128)S(1)} collective-permute-done((f32[12,2,512]{2,1,0:T(2,128)S(1)}, f32[12,2,512]{2,1,0:T(2,128)S(1)}, u32[]{:S(2)}, u32[]{:S(2)}) %collective-permute-start.3) | collective-permute-done | bytes 49184 | tf_op jit(solution)/shard_map/ppermute | solution.py:29
  183.2 10.6 %convolution_add_fusion.4 = f32[8,32,512]{2,1,0:T(8,128)S(1)} fusion(f32[8,32,256]{2,1,0:T(8,128)S(1)} %convolution_bitcast_fusion, f32[12,36,516]{2,1,0:T(8,128)S(1)} %select_maximum_fusion.4, f32[12,34,512]{2,1,0:T(8,128)S(1)} %get-tuple-element.29, f32[2,32,512]{2,1,0:T(8,128)S(1)} %collective-permute-done.1, f32[8,32,512]{2,1,0:T(8,128)S(1)} %bitcast.88, ...), kind=kOutput, calls=%fused_computation.255 | convolution fusion | flops 436600832 | bytes 64495616 | tf_op jit(solution)/shard_map/fc,abc->abf/dot_general | solution.py:94
  199.2 4.3 %collective-permute-start.21 = (f32[2,32,512]{2,1,0:T(8,128)S(1)}, f32[2,32,512]{2,1,0:T(8,128)S(1)}, u32[]{:S(2)}, u32[]{:S(2)}) collective-permute-start(f32[2,32,512]{2,1,0:T(8,128)S(1)} %get-tuple-element.32), channel_id=1, source_target_pairs={{0,4},{4,8},{8,12},{12,16},{16,20},{20,24},{24,28},{1,5},{5,9},{9,... | collective-permute-start | bytes 393224 | tf_op jit(solution)/shard_map/ppermute | solution.py:27
  204.0 2.9 %collective-permute-done.21 = f32[2,32,512]{2,1,0:T(8,128)S(1)} collective-permute-done((f32[2,32,512]{2,1,0:T(8,128)S(1)}, f32[2,32,512]{2,1,0:T(8,128)S(1)}, u32[]{:S(2)}, u32[]{:S(2)}) %collective-permute-start.21) | collective-permute-done | bytes 131104 | tf_op jit(solution)/shard_map/ppermute | solution.py:27
  209.3 3.3 %collective-permute-start.23 = (f32[12,2,512]{2,1,0:T(2,128)S(1)}, f32[12,2,512]{2,1,0:T(2,128)S(1)}, u32[]{:S(2)}, u32[]{:S(2)}) collective-permute-start(f32[12,2,512]{2,1,0:T(2,128)S(1)} %get-tuple-element.26), channel_id=1, source_target_pairs={{0,1},{1,2},{2,3},{4,5},{5,6},{6,7},{8,9},{9,10},{10,11},{12,13},{... | collective-permute-start | bytes 147464 | tf_op jit(solution)/shard_map/ppermute | solution.py:27
  216.1 17.7 %shard_map.42 = f32[3,8192]{1,0:T(4,128)} custom-call(s32[3,8192]{1,0:T(4,128)S(1)} %copy-done.1, f32[1,8192]{1,0:T(1,128)S(1)} %bitcast.91, f32[768,512]{1,0:T(8,128)S(1)} %bitcast.89), custom_call_target="tpu_custom_call" | custom-call | tf_op jit(solution)/shard_map/pallas_call | solution.py:212
  (149 shorter events, 52.0 us)
Async XLA Ops:
  62.8 61.1 %collective-permute-start.12 = (f32[2,8,128]{2,1,0:T(8,128)S(1)}, f32[2,8,128]{2,1,0:T(8,128)S(1)}, u32[]{:S(2)}, u32[]{:S(2)}) collective-permute-start(f32[2,8,128]{2,1,0:T(8,128)S(1)} %reduce_sum.91), channel_id=1, source_target_pairs={{0,4},{4,8},{8,12},{12,16},{16,20},{20,24},{24,28},{1,5},{5,9},{9,... | collective-permute-start | bytes 24584 | tf_op jit(solution)/shard_map/ppermute | solution.py:27
  66.0 57.9 %collective-permute-start.13 = (f32[2,8,128]{2,1,0:T(8,128)S(1)}, f32[2,8,128]{2,1,0:T(8,128)S(1)}, u32[]{:S(2)}, u32[]{:S(2)}) collective-permute-start(f32[2,8,128]{2,1,0:T(8,128)S(1)} %reduce_sum.91), channel_id=1, source_target_pairs={{4,0},{8,4},{12,8},{16,12},{20,16},{24,20},{28,24},{5,1},{9,5},{13... | collective-permute-start | bytes 24584 | tf_op jit(solution)/shard_map/ppermute | solution.py:29
  68.2 74.3 %collective-permute-start.4 = (f32[2,16,256]{2,0,1:T(2,128)S(1)}, f32[2,16,256]{2,0,1:T(2,128)S(1)}, u32[]{:S(2)}, u32[]{:S(2)}) collective-permute-start(f32[2,16,256]{2,0,1:T(2,128)S(1)} %get-tuple-element.44), channel_id=1, source_target_pairs={{0,4},{4,8},{8,12},{12,16},{16,20},{20,24},{24,28},{1,5},{5,9},{9,... | collective-permute-start | bytes 98312 | tf_op jit(solution)/shard_map/ppermute | solution.py:27
  72.3 72.4 %collective-permute-start.5 = (f32[2,16,256]{2,0,1:T(2,128)S(1)}, f32[2,16,256]{2,0,1:T(2,128)S(1)}, u32[]{:S(2)}, u32[]{:S(2)}) collective-permute-start(f32[2,16,256]{2,0,1:T(2,128)S(1)} %get-tuple-element.45), channel_id=1, source_target_pairs={{4,0},{8,4},{12,8},{16,12},{20,16},{24,20},{28,24},{5,1},{9,5},{13... | collective-permute-start | bytes 98312 | tf_op jit(solution)/shard_map/ppermute | solution.py:29
  74.2 100.7 %collective-permute-start = (f32[2,32,512]{2,1,0:T(8,128)S(1)}, f32[2,32,512]{2,1,0:T(8,128)S(1)}, u32[]{:S(2)}, u32[]{:S(2)}) collective-permute-start(f32[2,32,512]{2,1,0:T(8,128)S(1)} %bitcast.96), channel_id=1, source_target_pairs={{0,4},{4,8},{8,12},{12,16},{16,20},{20,24},{24,28},{1,5},{5,9},{9,... | collective-permute-start | bytes 393224 | tf_op jit(solution)/shard_map/ppermute | solution.py:27
  124.0 4.4 %collective-permute-start.14 = (f32[6,2,128]{2,1,0:T(2,128)S(1)}, f32[6,2,128]{2,1,0:T(2,128)S(1)}, u32[]{:S(2)}, u32[]{:S(2)}) collective-permute-start(f32[6,2,128]{2,1,0:T(2,128)S(1)} %get-tuple-element.48), channel_id=1, source_target_pairs={{0,1},{1,2},{2,3},{4,5},{5,6},{6,7},{8,9},{9,10},{10,11},{12,13},{... | collective-permute-start | bytes 18440 | tf_op jit(solution)/shard_map/ppermute | solution.py:27
  125.9 4.9 %collective-permute-start.15 = (f32[6,2,128]{2,1,0:T(2,128)S(1)}, f32[6,2,128]{2,1,0:T(2,128)S(1)}, u32[]{:S(2)}, u32[]{:S(2)}) collective-permute-start(f32[6,2,128]{2,1,0:T(2,128)S(1)} %get-tuple-element.49), channel_id=1, source_target_pairs={{1,0},{2,1},{3,2},{5,4},{6,5},{7,6},{9,8},{10,9},{11,10},{13,12},{... | collective-permute-start | bytes 18440 | tf_op jit(solution)/shard_map/ppermute | solution.py:29
  131.2 7.1 %collective-permute-start.16 = (f32[1,8,128]{2,1,0:T(8,128)S(1)}, f32[1,8,128]{2,1,0:T(8,128)S(1)}, u32[]{:S(2)}, u32[]{:S(2)}) collective-permute-start(f32[1,8,128]{2,1,0:T(8,128)S(1)} %get-tuple-element.52), channel_id=1, source_target_pairs={{0,4},{4,8},{8,12},{12,16},{16,20},{20,24},{24,28},{1,5},{5,9},{9,... | collective-permute-start | bytes 12296 | tf_op jit(solution)/shard_map/ppermute | solution.py:27
  133.1 7.1 %collective-permute-start.17 = (f32[1,8,128]{2,1,0:T(8,128)S(1)}, f32[1,8,128]{2,1,0:T(8,128)S(1)}, u32[]{:S(2)}, u32[]{:S(2)}) collective-permute-start(f32[1,8,128]{2,1,0:T(8,128)S(1)} %get-tuple-element.53), channel_id=1, source_target_pairs={{4,0},{8,4},{12,8},{16,12},{20,16},{24,20},{28,24},{5,1},{9,5},{13... | collective-permute-start | bytes 12296 | tf_op jit(solution)/shard_map/ppermute | solution.py:29
  138.3 36.6 %collective-permute-start.1 = (f32[2,32,512]{2,1,0:T(8,128)S(1)}, f32[2,32,512]{2,1,0:T(8,128)S(1)}, u32[]{:S(2)}, u32[]{:S(2)}) collective-permute-start(f32[2,32,512]{2,1,0:T(8,128)S(1)} %bitcast.95), channel_id=1, source_target_pairs={{4,0},{8,4},{12,8},{16,12},{20,16},{24,20},{28,24},{5,1},{9,5},{13... | collective-permute-start | bytes 393224 | tf_op jit(solution)/shard_map/ppermute | solution.py:29
  140.3 7.9 %collective-permute-start.18 = (f32[4,1,128]{2,1,0:T(1,128)S(1)}, f32[4,1,128]{2,1,0:T(1,128)S(1)}, u32[]{:S(2)}, u32[]{:S(2)}) collective-permute-start(f32[4,1,128]{2,1,0:T(1,128)S(1)} %get-tuple-element.50), channel_id=1, source_target_pairs={{0,1},{1,2},{2,3},{4,5},{5,6},{6,7},{8,9},{9,10},{10,11},{12,13},{... | collective-permute-start | bytes 6152 | tf_op jit(solution)/shard_map/ppermute | solution.py:27
  142.5 7.7 %collective-permute-start.19 = (f32[4,1,128]{2,1,0:T(1,128)S(1)}, f32[4,1,128]{2,1,0:T(1,128)S(1)}, u32[]{:S(2)}, u32[]{:S(2)}) collective-permute-start(f32[4,1,128]{2,1,0:T(1,128)S(1)} %get-tuple-element.51), channel_id=1, source_target_pairs={{1,0},{2,1},{3,2},{5,4},{6,5},{7,6},{9,8},{10,9},{11,10},{13,12},{... | collective-permute-start | bytes 6152 | tf_op jit(solution)/shard_map/ppermute | solution.py:29
  144.7 5.6 %collective-permute-start.6 = (f32[8,2,256]{2,0,1:T(8,128)S(1)}, f32[8,2,256]{2,0,1:T(8,128)S(1)}, u32[]{:S(2)}, u32[]{:S(2)}) collective-permute-start(f32[8,2,256]{2,0,1:T(8,128)S(1)} %get-tuple-element.38), channel_id=1, source_target_pairs={{0,1},{1,2},{2,3},{4,5},{5,6},{6,7},{8,9},{9,10},{10,11},{12,13},{... | collective-permute-start | bytes 49160 | tf_op jit(solution)/shard_map/ppermute | solution.py:27
  148.2 5.1 %collective-permute-start.7 = (f32[8,2,256]{2,0,1:T(8,128)S(1)}, f32[8,2,256]{2,0,1:T(8,128)S(1)}, u32[]{:S(2)}, u32[]{:S(2)}) collective-permute-start(f32[8,2,256]{2,0,1:T(8,128)S(1)} %get-tuple-element.39), channel_id=1, source_target_pairs={{1,0},{2,1},{3,2},{5,4},{6,5},{7,6},{9,8},{10,9},{11,10},{13,12},{... | collective-permute-start | bytes 49160 | tf_op jit(solution)/shard_map/ppermute | solution.py:29
  156.3 6.7 %collective-permute-start.8 = (f32[1,16,256]{2,0,1:T(1,128)S(1)}, f32[1,16,256]{2,0,1:T(1,128)S(1)}, u32[]{:S(2)}, u32[]{:S(2)}) collective-permute-start(f32[1,16,256]{2,0,1:T(1,128)S(1)} %get-tuple-element.42), channel_id=1, source_target_pairs={{0,4},{4,8},{8,12},{12,16},{16,20},{20,24},{24,28},{1,5},{5,9},{9,... | collective-permute-start | bytes 49160 | tf_op jit(solution)/shard_map/ppermute | solution.py:27
  160.9 5.4 %collective-permute-start.9 = (f32[1,16,256]{2,0,1:T(1,128)S(1)}, f32[1,16,256]{2,0,1:T(1,128)S(1)}, u32[]{:S(2)}, u32[]{:S(2)}) collective-permute-start(f32[1,16,256]{2,0,1:T(1,128)S(1)} %get-tuple-element.43), channel_id=1, source_target_pairs={{4,0},{8,4},{12,8},{16,12},{20,16},{24,20},{28,24},{5,1},{9,5},{13... | collective-permute-start | bytes 49160 | tf_op jit(solution)/shard_map/ppermute | solution.py:29
  166.3 5.6 %collective-permute-start.10 = (f32[6,1,256]{2,0,1:T(8,128)S(1)}, f32[6,1,256]{2,0,1:T(8,128)S(1)}, u32[]{:S(2)}, u32[]{:S(2)}) collective-permute-start(f32[6,1,256]{2,0,1:T(8,128)S(1)} %get-tuple-element.40), channel_id=1, source_target_pairs={{0,1},{1,2},{2,3},{4,5},{5,6},{6,7},{8,9},{9,10},{10,11},{12,13},{... | collective-permute-start | bytes 18440 | tf_op jit(solution)/shard_map/ppermute | solution.py:27
  169.6 5.0 %collective-permute-start.11 = (f32[6,1,256]{2,0,1:T(8,128)S(1)}, f32[6,1,256]{2,0,1:T(8,128)S(1)}, u32[]{:S(2)}, u32[]{:S(2)}) collective-permute-start(f32[6,1,256]{2,0,1:T(8,128)S(1)} %get-tuple-element.41), channel_id=1, source_target_pairs={{1,0},{2,1},{3,2},{5,4},{6,5},{7,6},{9,8},{10,9},{11,10},{13,12},{... | collective-permute-start | bytes 18440 | tf_op jit(solution)/shard_map/ppermute | solution.py:29
  175.0 4.8 %collective-permute-start.2 = (f32[12,2,512]{2,1,0:T(2,128)S(1)}, f32[12,2,512]{2,1,0:T(2,128)S(1)}, u32[]{:S(2)}, u32[]{:S(2)}) collective-permute-start(f32[12,2,512]{2,1,0:T(2,128)S(1)} %get-tuple-element.30), channel_id=1, source_target_pairs={{0,1},{1,2},{2,3},{4,5},{5,6},{6,7},{8,9},{9,10},{10,11},{12,13},{... | collective-permute-start | bytes 147464 | tf_op jit(solution)/shard_map/ppermute | solution.py:27
  177.0 5.4 %collective-permute-start.3 = (f32[12,2,512]{2,1,0:T(2,128)S(1)}, f32[12,2,512]{2,1,0:T(2,128)S(1)}, u32[]{:S(2)}, u32[]{:S(2)}) collective-permute-start(f32[12,2,512]{2,1,0:T(2,128)S(1)} %get-tuple-element.31), channel_id=1, source_target_pairs={{1,0},{2,1},{3,2},{5,4},{6,5},{7,6},{9,8},{10,9},{11,10},{13,12},{... | collective-permute-start | bytes 147464 | tf_op jit(solution)/shard_map/ppermute | solution.py:29
  197.2 6.8 %collective-permute-start.20 = (f32[2,32,512]{2,1,0:T(8,128)S(1)}, f32[2,32,512]{2,1,0:T(8,128)S(1)}, u32[]{:S(2)}, u32[]{:S(2)}) collective-permute-start(f32[2,32,512]{2,1,0:T(8,128)S(1)} %get-tuple-element.33), channel_id=1, source_target_pairs={{4,0},{8,4},{12,8},{16,12},{20,16},{24,20},{28,24},{5,1},{9,5},{13... | collective-permute-start | bytes 393224 | tf_op jit(solution)/shard_map/ppermute | solution.py:29
  199.2 7.7 %collective-permute-start.21 = (f32[2,32,512]{2,1,0:T(8,128)S(1)}, f32[2,32,512]{2,1,0:T(8,128)S(1)}, u32[]{:S(2)}, u32[]{:S(2)}) collective-permute-start(f32[2,32,512]{2,1,0:T(8,128)S(1)} %get-tuple-element.32), channel_id=1, source_target_pairs={{0,4},{4,8},{8,12},{12,16},{16,20},{20,24},{24,28},{1,5},{5,9},{9,... | collective-permute-start | bytes 393224 | tf_op jit(solution)/shard_map/ppermute | solution.py:27
  207.0 5.7 %collective-permute-start.22 = (f32[12,2,512]{2,1,0:T(2,128)S(1)}, f32[12,2,512]{2,1,0:T(2,128)S(1)}, u32[]{:S(2)}, u32[]{:S(2)}) collective-permute-start(f32[12,2,512]{2,1,0:T(2,128)S(1)} %get-tuple-element.27), channel_id=1, source_target_pairs={{1,0},{2,1},{3,2},{5,4},{6,5},{7,6},{9,8},{10,9},{11,10},{13,12},{... | collective-permute-start | bytes 147464 | tf_op jit(solution)/shard_map/ppermute | solution.py:29
  209.3 4.4 %collective-permute-start.23 = (f32[12,2,512]{2,1,0:T(2,128)S(1)}, f32[12,2,512]{2,1,0:T(2,128)S(1)}, u32[]{:S(2)}, u32[]{:S(2)}) collective-permute-start(f32[12,2,512]{2,1,0:T(2,128)S(1)} %get-tuple-element.26), channel_id=1, source_target_pairs={{0,1},{1,2},{2,3},{4,5},{5,6},{6,7},{8,9},{9,10},{10,11},{12,13},{... | collective-permute-start | bytes 147464 | tf_op jit(solution)/shard_map/ppermute | solution.py:27
  (5 other events, 21.0 us)

commit v2 on v1

v2 whole, which is shorter than its diff:
```python
import functools
import math

import jax
import jax.numpy as jnp
import numpy as np
from jax import lax
from jax.experimental import pallas as pl
from jax.experimental.pallas import tpu as pltpu
from jax.sharding import PartitionSpec as P

CZ = 8
CY = 32
NX = 512
F = 32
ROWS = CZ * CY
CHUNK = 1024
MESH = pl.DeviceIdType.MESH
HIGHEST = lax.Precision.HIGHEST
VMEM = pl.BlockSpec(memory_space=pltpu.VMEM)
SQUARES = (0, 1, 2, 4, 5, 8)


def iota(shape, dim):
    return lax.broadcasted_iota(jnp.int32, shape, dim)


def near_weight(squared):
    return 1.0 / math.sqrt(squared + 0.25) - 1.0 / math.sqrt(squared + 4.0)


def level_weight(level, squared):
    return (1.0 / math.sqrt(squared + 1.0) - 1.0 / math.sqrt(squared + 4.0)) / 2**level


def dot32(left, right):
    return jnp.dot(left, right, precision=HIGHEST, preferred_element_type=jnp.float32)


def split_two(values):
    high = values.astype(jnp.bfloat16)
    return high, (values - high.astype(jnp.float32)).astype(jnp.bfloat16)


def local_rows(cell_ref, start, width):
    z0 = lax.axis_index("slab") * CZ
    y0 = lax.axis_index("pencil") * CY
    plane = cell_ref[0:1, pl.ds(start, width)] - z0
    line = cell_ref[1:2, pl.ds(start, width)] - y0
    return plane * CY + line, cell_ref[2:3, pl.ds(start, width)]


def halve_rows(rows_out, rows_in, line_bits):
    out_row = iota((rows_out, rows_in), 0)
    in_row = iota((rows_out, rows_in), 1)
    plane = in_row >> (line_bits + 1)
    line = (in_row & (2**line_bits - 1)) >> 1
    return jnp.where((plane << (line_bits - 1)) + line == out_row, 1.0, 0.0)


def halve_columns(columns_in, columns_out):
    return jnp.where(
        iota((columns_in, columns_out), 0) >> 1 == iota((columns_in, columns_out), 1), 1.0, 0.0
    )


def deposit_kernel(cell_ref, charge_ref, grid_ref, one_ref, two_ref, three_ref, total_ref):
    atoms = cell_ref.shape[1]
    width = math.gcd(atoms, CHUNK)
    total_ref[...] = jnp.zeros_like(total_ref)

    @pl.loop(0, atoms // width)
    def _(step):
        start = pl.multiple_of(step * width, width)
        rows, columns = local_rows(cell_ref, start, width)
        charges = charge_ref[:, pl.ds(start, width)]
        high = charges.astype(jnp.bfloat16).astype(jnp.float32)
        low = charges - high
        at_row = iota((ROWS, width), 0) == rows
        table = jnp.where(iota((NX, width), 0) == columns, 1.0, 0.0).astype(jnp.bfloat16)
        stacked = jnp.concatenate(
            [
                jnp.where(at_row, high, 0.0).astype(jnp.bfloat16),
                jnp.where(at_row, low, 0.0).astype(jnp.bfloat16),
            ],
            axis=0,
        )
        added = lax.dot_general(
            stacked, table, (((1,), (1,)), ((), ())), preferred_element_type=jnp.float32
        )
        total_ref[...] += added[:ROWS] + added[ROWS:]

    grid = total_ref[...]
    grid_ref[...] = grid.reshape(CZ, CY, NX)
    one = dot32(dot32(halve_rows(ROWS // 4, ROWS, 5), grid), halve_columns(NX, NX // 2))
    one_ref[...] = one.reshape(CZ // 2, CY // 2, NX // 2)
    two = dot32(
        dot32(halve_rows(ROWS // 16, ROWS // 4, 4), one), halve_columns(NX // 2, NX // 4)
    )
    two_ref[...] = two.reshape(CZ // 4, CY // 4, NX // 4)
    three_ref[...] = dot32(
        dot32(halve_rows(8, ROWS // 16, 3), two), halve_columns(NX // 4, NX // 4)
    )


def deposit_call(atom_cell, charge):
    shapes = ((CZ, CY, NX), (CZ // 2, CY // 2, NX // 2), (CZ // 4, CY // 4, NX // 4), (8, 128))
    return pl.pallas_call(
        deposit_kernel,
        out_shape=[jax.ShapeDtypeStruct(shape, jnp.float32) for shape in shapes],
        in_specs=[VMEM] * 2,
        out_specs=[VMEM] * 4,
        scratch_shapes=[pltpu.VMEM((ROWS, NX), jnp.float32)],
        compiler_params=pltpu.CompilerParams(vmem_limit_bytes=48 * 2**20),
    )(atom_cell, charge.reshape(1, -1))


def window(level, dz, dy):
    if level == 0:
        z = {1: (4, 0, 4), -1: (0, 12, 4), 0: (0, 4, 8)}[dz]
        y = {1: (24, 0, 8), -1: (0, 40, 8), 0: (0, 8, 32)}[dy]
    elif level == 1:
        z = {1: (0, 0, 4), -1: (0, 8, 4), 0: (0, 4, 4)}[dz]
        y = {1: (8, 0, 8), -1: (0, 24, 8), 0: (0, 8, 16)}[dy]
    else:
        z = (0, 4 - 2 * dz, 2)
        y = (0, 8 - 8 * dy, 8)
    return z, y


def exchange_kernel(
    slabs, pencils, zero, one, two, three, wide0, wide1, wide2, wide3, send, recv, send3, recv3
):
    slab = lax.axis_index("slab")
    pencil = lax.axis_index("pencil")
    devices = slabs * pencils
    me = slab * pencils + pencil
    for ref in (wide0, wide1, wide2):
        ref[...] = jnp.zeros_like(ref)
    wide0[4:12, 8:40, :] = zero[...]
    wide1[4:8, 8:24, :] = one[...]
    wide2[4:6, 8:16, :] = two[...]
    wide3[pl.ds(me, 1)] = three[...][None]

    def place(step):
        other = lax.rem(me + step, devices)
        return (other // pencils, lax.rem(other, pencils))

    barrier = pltpu.get_barrier_semaphore()

    @pl.loop(1, devices)
    def _(step):
        pl.semaphore_signal(barrier, inc=1, device_id=place(step), device_id_type=MESH)

    pl.semaphore_wait(barrier, devices - 1)

    offsets = [(0, dz, dy) for dz in (-1, 0, 1) for dy in (-1, 0, 1) if dz or dy]
    offsets += [(1, dz, dy) for dz in (-1, 0, 1) for dy in (-1, 0, 1) if dz or dy]
    offsets += [(2, dz, dy) for dz in range(-2, 3) for dy in (-1, 0, 1) if dz or dy]
    sources = (zero, one, two)
    targets = (wide0, wide1, wide2)

    def inside(dz, dy):
        z = slab + dz
        y = pencil + dy
        return (z >= 0) & (z < slabs) & (y >= 0) & (y < pencils)

    def copy_of(index, device):
        level, dz, dy = offsets[index]
        (zs, zd, zn), (ys, yd, yn) = window(level, dz, dy)
        return pltpu.make_async_remote_copy(
            src_ref=sources[level].at[pl.ds(zs, zn), pl.ds(ys, yn), :],
            dst_ref=targets[level].at[pl.ds(zd, zn), pl.ds(yd, yn), :],
            send_sem=send.at[index],
            recv_sem=recv.at[index],
            device_id=device,
            device_id_type=MESH,
        )

    def top_copy(step, slot):
        return pltpu.make_async_remote_copy(
            src_ref=three,
            dst_ref=wide3.at[slot],
            send_sem=send3.at[step],
            recv_sem=recv3.at[step],
            device_id=place(step),
            device_id_type=MESH,
        )

    for index, (level, dz, dy) in enumerate(offsets):

        @pl.when(inside(dz, dy))
        def _():
            copy_of(index, (slab + dz, pencil + dy)).start()

    @pl.loop(1, devices)
    def _(step):
        top_copy(step, me).start()

    @pl.loop(1, devices)
    def _(step):
        copy = top_copy(step, lax.rem(me + devices - step, devices))
        copy.wait_send()
        copy.wait_recv()

    for index, (level, dz, dy) in enumerate(offsets):

        @pl.when(inside(-dz, -dy))
        def _():
            copy_of(index, (slab - dz, pencil - dy)).wait_recv()

        @pl.when(inside(dz, dy))
        def _():
            copy_of(index, (slab + dz, pencil + dy)).wait_send()


def exchange_call(slabs, pencils, parts):
    devices = slabs * pencils
    shapes = ((16, 48, NX), (12, 32, NX // 2), (10, 32, NX // 4), (devices, 8, 128))
    return pl.pallas_call(
        functools.partial(exchange_kernel, slabs, pencils),
        out_shape=[jax.ShapeDtypeStruct(shape, jnp.float32) for shape in shapes],
        in_specs=[VMEM] * 4,
        out_specs=[VMEM] * 4,
        scratch_shapes=[
            pltpu.SemaphoreType.DMA((30,)),
            pltpu.SemaphoreType.DMA((30,)),
            pltpu.SemaphoreType.DMA((devices,)),
            pltpu.SemaphoreType.DMA((devices,)),
        ],
        compiler_params=pltpu.CompilerParams(
            collective_id=0, has_side_effects=True, vmem_limit_bytes=48 * 2**20
        ),
    )(*parts)


def shift_x(values, step):
    width = values.shape[-1]
    axis = values.ndim - 1
    column = iota(values.shape, axis)
    moved = pltpu.roll(values, (-step) % width, axis)
    return jnp.where((column + step >= 0) & (column + step < width), moved, 0.0)


def pair_x(values, step):
    return shift_x(values, step) + shift_x(values, -step)


def hat(fine, cell, factor, count):
    bits = factor.bit_length()
    numerator = jnp.clip(2 * fine + 1 - factor, 0, 2 * factor * (count - 1))
    lower = jnp.minimum(numerator >> bits, count - 2)
    fraction = (numerator - (lower << bits)).astype(jnp.float32) * (0.5 / factor)
    return jnp.where(
        cell == lower, 1.0 - fraction, jnp.where(cell == lower + 1, fraction, 0.0)
    )


def window_stencil(level, planes_in, planes_out, lines, shift):
    blocks = []
    dz = np.arange(planes_in)[None, :] - np.arange(planes_out)[:, None] + shift
    dy = np.arange(lines)[None, :] - np.arange(lines)[:, None]
    dz = dz[:, None, :, None]
    dy = dy[None, :, None, :]
    near = (np.abs(dz) <= 2) & (np.abs(dy) <= 2)
    for c in range(3):
        squared = (dz * dz + dy * dy + c * c).astype(np.float64)
        weight = (1.0 / np.sqrt(squared + 1.0) - 1.0 / np.sqrt(squared + 4.0)) / 2**level
        weight = np.where(near, weight, 0.0)
        blocks.append(weight.reshape(planes_out * lines, planes_in * lines))
    return np.concatenate(blocks, axis=1).astype(np.float32)


def field_kernel(
    slabs,
    pencils,
    cell_ref,
    charge_ref,
    wide0,
    wide1,
    wide2,
    wide3,
    stencil1,
    stencil2,
    pot_ref,
    force_ref,
    sums,
    wide_pot,
    field1,
    field2,
    field3,
    along_x,
    high_ref,
    low_ref,
):
    slab = lax.axis_index("slab")
    pencil = lax.axis_index("pencil")
    pencil_bits = pencils.bit_length() - 1

    grid1 = wide1[...].reshape(12 * 32, NX // 2)
    field1[...] = dot32(
        stencil1[...], jnp.concatenate([grid1, pair_x(grid1, 1), pair_x(grid1, 2)], axis=0)
    )
    grid2 = wide2[...].reshape(10 * 32, NX // 4)
    field2[...] = dot32(
        stencil2[...], jnp.concatenate([grid2, pair_x(grid2, 1), pair_x(grid2, 2)], axis=0)
    )
    rows3 = slabs * pencils * 8
    grid3 = wide3[...].reshape(rows3, 128)
    coarse = []
    first_row = 0
    first_lane = 0
    for level in (3, 4, 5):
        down = level - 3
        line_bits = pencil_bits + 2 - down
        lines = 2**line_bits
        planes = slabs >> down
        count = planes * lines
        length = NX >> level
        shape = (count, rows3)
        out_row = iota(shape, 0)
        in_row = iota(shape, 1)
        in_plane = in_row >> (3 + pencil_bits)
        in_line = (((in_row >> 3) & (pencils - 1)) << 2) + (in_row & 7)
        cell = ((in_plane >> down) << line_bits) + (in_line >> down)
        chosen = jnp.where((cell == out_row) & ((in_row & 7) < 4), 1.0, 0.0)
        charges = dot32(chosen, grid3)
        reach = 3 if level < 5 else length
        source = iota((128, 128), 0) >> down
        column = iota((128, 128), 1) - first_lane
        valid = (column >= 0) & (column < length)
        pairs = jnp.concatenate(
            [
                jnp.where(valid & (jnp.abs(source - column) == c), 1.0, 0.0)
                for c in range(reach)
            ],
            axis=1,
        )
        moved = dot32(charges, pairs)
        stacked = jnp.concatenate(
            [moved[:, c * 128 : (c + 1) * 128] for c in range(reach)], axis=0
        )
        blocks = []
        for c in range(reach):
            shape = (4 * lines, count)
            dz = (iota(shape, 1) >> line_bits) - (iota(shape, 0) >> line_bits)
            dz = dz - ((slab >> down) - 1)
            dy = (iota(shape, 1) & (lines - 1)) - (iota(shape, 0) & (lines - 1))
            squared = dz * dz + dy * dy
            if level < 5:
                weight = jnp.zeros(shape, jnp.float32)
                for value in SQUARES:
                    weight = jnp.where(
                        squared == value, level_weight(level, value + c * c), weight
                    )
                weight = jnp.where((jnp.abs(dz) <= 2) & (jnp.abs(dy) <= 2), weight, 0.0)
            else:
                weight = (1.0 / F) / jnp.sqrt((squared + (c * c + 1)).astype(jnp.float32))
            blocks.append(dot32(weight, stacked[c * count : (c + 1) * count]))
        field3[first_row : first_row + 4 * lines, :] = sum(blocks[1:], blocks[0])
        first_row = first_row + 4 * lines
        first_lane = first_lane + length

    lane = 0
    for level in range(1, 6):
        length = NX >> level
        rows = length if level < 5 else NX - lane
        weights = hat(iota((rows, NX), 1), iota((rows, NX), 0), 2**level, length)
        weights = jnp.where(iota((rows, NX), 0) < length, weights, 0.0)
        along_x[lane : lane + rows, :] = weights.astype(jnp.bfloat16)
        lane = lane + rows

    @pl.loop(0, 4)
    def _(step):

        def along_zy(level, planes, lines, plane0, line0):
            shape = (3, 48, planes * lines)
            bits = lines.bit_length() - 1
            fine_z = CZ * slab - 2 + 3 * step + iota(shape, 0)
            fine_y = CY * pencil - 8 + iota(shape, 1)
            plane = plane0 + (iota(shape, 2) >> bits)
            line = line0 + (iota(shape, 2) & (lines - 1))
            weights = hat(fine_z, plane, 2**level, (slabs * CZ) >> level) * hat(
                fine_y, line, 2**level, (pencils * CY) >> level
            )
            return weights.reshape(3 * 48, planes * lines)

        parts = [
            dot32(along_zy(1, 8, 32, 4 * slab - 2, 16 * pencil - 8), field1[...]),
            dot32(along_zy(2, 4, 32, 2 * slab - 1, 8 * pencil - 8), field2[...]),
        ]
        first_row = 0
        last = jnp.zeros((3 * 48, 128), jnp.float32)
        for level in (3, 4, 5):
            lines = (pencils * CY) >> level
            weights = along_zy(level, 4, lines, (slab >> (level - 3)) - 1, 0)
            last = last + dot32(weights, field3[first_row : first_row + 4 * lines, :])
            first_row = first_row + 4 * lines
        parts.append(last)
        high, low = split_two(jnp.concatenate(parts, axis=1))
        fine = jnp.dot(high, along_x[...], preferred_element_type=jnp.float32)
        fine += jnp.dot(low, along_x[...], preferred_element_type=jnp.float32)
        wide_pot[pl.ds(4 + 3 * step, 3)] = fine.reshape(3, 48, NX)

    for edge in (0, 1, 2, 3, 16, 17, 18, 19):
        wide_pot[edge] = jnp.zeros((48, NX), jnp.float32)

    @pl.loop(0, 16)
    def _(plane):
        values = wide0[plane]
        sums[0] = values
        sums[1] = pair_x(values, 1)
        sums[2] = pair_x(values, 2)
        for block in range(NX // 128):
            lanes = pl.ds(block * 128, 128)
            table = {}
            for c in range(3):
                part = sums[c, :, lanes]
                table[0, c] = part
                for b in (1, 2):
                    table[b, c] = pltpu.roll(part, b, 0) + pltpu.roll(part, 48 - b, 0)
            groups = {
                0: table[0, 0],
                1: table[0, 1] + table[1, 0],
                2: table[1, 1],
                4: table[0, 2] + table[2, 0],
                5: table[1, 2] + table[2, 1],
                8: table[2, 2],
            }
            for a in range(3):
                total = sum(near_weight(a * a + k) * groups[k] for k in SQUARES)
                for target in {a, -a}:
                    wide_pot[plane + 2 + target, :, lanes] += total

    @pl.loop(0, 12)
    def _(plane):
        shape = (48, NX)
        row = CY * pencil - 8 + iota(shape, 0)
        whole_plane = CZ * slab - 2 + plane + jnp.zeros(shape, jnp.int32)
        valid = (row >= 0) & (row < pencils * CY)
        valid = valid & (whole_plane >= 0) & (whole_plane < slabs * CZ)
        wide_pot[plane + 4] = jnp.where(valid, wide_pot[plane + 4], 0.0)

    def slope(after1, before1, after2, before2):
        return (8.0 * (after1 - before1) - (after2 - before2)) * (1.0 / 12.0)

    @pl.loop(0, CZ)
    def _(plane):
        middle = wide_pot[plane + 6]
        own = middle[8:40]
        pot_ref[plane] = own
        at = [wide_pot[plane + 6 + k, 8:40, :] for k in (1, -1, 2, -2)]
        across = [pltpu.roll(middle, (-k) % 48, 0)[8:40] for k in (1, -1, 2, -2)]
        along = [shift_x(own, k) for k in (1, -1, 2, -2)]
        for direction, four in enumerate((at, across, along)):
            high, low = split_two(slope(*four))
            start = pl.multiple_of(direction * ROWS + plane * CY, CY)
            high_ref[pl.ds(start, CY), :] = high
            low_ref[pl.ds(start, CY), :] = low

    atoms = cell_ref.shape[1]
    width = math.gcd(atoms, 512)

    @pl.loop(0, atoms // width)
    def _(step):
        start = pl.multiple_of(step * width, width)
        rows, columns = local_rows(cell_ref, start, width)
        charges = charge_ref[:, pl.ds(start, width)]
        at_row = iota((ROWS, width), 0) == rows
        table = jnp.where(iota((NX, width), 0) == columns, 1.0, 0.0).astype(jnp.bfloat16)
        for direction in range(3):
            part = pl.ds(direction * ROWS, ROWS)
            at_cell = jnp.dot(high_ref[part, :], table, preferred_element_type=jnp.float32)
            at_cell += jnp.dot(low_ref[part, :], table, preferred_element_type=jnp.float32)
            chosen = jnp.sum(jnp.where(at_row, at_cell, 0.0), axis=0, keepdims=True)
            force_ref[direction : direction + 1, pl.ds(start, width)] = -charges * chosen


def field_call(slabs, pencils, atom_cell, charge, wide):
    stencil1 = window_stencil(1, 12, 8, 32, -2)
    stencil2 = window_stencil(2, 10, 4, 32, -3)
    field3_rows = sum(4 * ((pencils * CY) >> level) for level in (3, 4, 5))
    return pl.pallas_call(
        functools.partial(field_kernel, slabs, pencils),
        out_shape=[
            jax.ShapeDtypeStruct((CZ, CY, NX), jnp.float32),
            jax.ShapeDtypeStruct(atom_cell.shape, jnp.float32),
        ],
        in_specs=[VMEM] * 8,
        out_specs=[VMEM] * 2,
        scratch_shapes=[
            pltpu.VMEM((3, 48, NX), jnp.float32),
            pltpu.VMEM((20, 48, NX), jnp.float32),
            pltpu.VMEM((8 * 32, NX // 2), jnp.float32),
            pltpu.VMEM((4 * 32, NX // 4), jnp.float32),
            pltpu.VMEM((field3_rows, 128), jnp.float32),
            pltpu.VMEM((NX, NX), jnp.bfloat16),
            pltpu.VMEM((3 * ROWS, NX), jnp.bfloat16),
            pltpu.VMEM((3 * ROWS, NX), jnp.bfloat16),
        ],
        compiler_params=pltpu.CompilerParams(vmem_limit_bytes=56 * 2**20),
    )(
        atom_cell,
        charge.reshape(1, -1),
        *wide,
        jnp.asarray(stencil1),
        jnp.asarray(stencil2),
    )


def solution(mesh):
    slabs = mesh.shape["slab"]
    pencils = mesh.shape["pencil"]

    def body(atom_cell, charge):
        parts = deposit_call(atom_cell, charge)
        wide = exchange_call(slabs, pencils, parts)
        potential, forces = field_call(slabs, pencils, atom_cell, charge, wide)
        return (potential, forces)

    return jax.shard_map(
        body,
        mesh=mesh,
        in_specs=(P(None, ("slab", "pencil")), P(("slab", "pencil"))),
        out_specs=(P("slab", "pencil", None), P(None, ("slab", "pencil"))),
        check_vma=False,
    )
```

time: 235 us -> 80.3 us (0.34)
  starting transfers between devices: 66.6 us -> 0 us
  Pallas kernels: 23.7 us -> 74.6 us
  local copies, waits for them, and re-layouts: 45.4 us -> 4.87 us
  blocking collectives: 36.2 us -> 0 us
  other arithmetic: 21.8 us -> 0 us
  matrix products: 20 us -> 0 us
  waiting for transfers between devices: 18.5 us -> 0 us
    ppermute x24 -> x0, starting transfers between devices: 66.6 us -> none  [the longest x12 38.4 us: extended(): lax.ppermute(tail, axis, [(i, (i + 1) % count) for i in range(ends)])]
    pallas_call x2 -> x3, Pallas kernels: 23.7 us -> 74.6 us  [the longest x1 35.6 us: field_call(): pl.pallas_call(functools.partial(field_kernel, slabs, pencils), out_shape...]
    all_gather x1 -> x0, blocking collectives: 36.2 us -> none  [body(): gathered = lax.all_gather(packed, ('slab', 'pencil'), axis=0, tiled=True)]
    another operation x4 -> x0, local copies, waits for them, and re-layouts: 35.1 us -> none  [the longest x1 34.9 us: restrict(): grid.reshape(planes // 2, 2, rows // 2, 2, length // 2, 2)]
    dot_general x16 -> x0, matrix products: 20 us -> none  [the longest x5 14 us: to_fine(): jnp.einsum('fc,abc->abf', along_x, section, precision=lax.Precision.HIGHEST)]
    ppermute x24 -> x0, waiting for transfers between devices: 18.5 us -> none  [the longest x12 14.5 us: extended(): lax.ppermute(head, axis, [((i + 1) % count, i) for i in range(ends)])]
    reduce_sum x13 -> x0, other arithmetic: 15.2 us -> none  [the longest x4 14.4 us: restrict(): grid.reshape(planes // 2, 2, rows // 2, 2, length // 2, 2)]
    reshape x6 -> x0, local copies, waits for them, and re-layouts: 5.81 us -> none  [the longest x1 5.54 us: restrict(): grid.reshape(planes // 2, 2, rows // 2, 2, length // 2, 2)]
  transfers between devices with their start and end apart: 24 -> 0, of which waited for: 8 -> 0; matrix products, arithmetic and copies ran while one was open for 6% -> 0% of each run, Pallas kernels for 0% -> 0%
where the time goes in v2:
time: 80.3 us; the launch traced here: 80.1 us
  Pallas kernels  74.6 us (93%)
  local copies, waits for them, and re-layouts  4.87 us (6%)
    pallas_call x1, Pallas kernels, field_call(): pl.pallas_call(functools.partial(field_kernel, slabs, pencils), out_shape...  35.6 us
    pallas_call x1, Pallas kernels, exchange_call(): pl.pallas_call(functools.partial(exchange_kernel, slabs, pencils), out_sh...  31.4 us
    pallas_call x1, Pallas kernels, deposit_call(): pl.pallas_call(deposit_kernel, out_shape=[jax.ShapeDtypeStruct(shape, jnp...  7.59 us
    unnamed x12, local copies, waits for them, and re-layouts  4.87 us

profile of v2, /device:TPU:3, one launch (start us, length us, event | category | flops | bytes accessed | tf_op | source)
XLA Modules:
  0.0 80.1 jit_solution(15193721685283028979)
XLA Ops:
  0.6 0.0 copy-start.1
  0.6 0.9 %copy-done.1 = s32[3,8192]{1,0:T(4,128)S(1)} copy-done((s32[3,8192]{1,0:T(4,128)S(1)}, s32[3,8192]{1,0:T(4,128)}, u32[]{:S(2)}) %copy-start.1) | copy-done | bytes 98328
  1.5 0.0 copy-start.4
  1.5 0.8 copy-done.4
  2.3 7.6 %shard_map.59 = (f32[8,32,512]{2,1,0:T(8,128)S(1)}, f32[4,16,256]{2,1,0:T(8,128)S(1)}, f32[2,8,128]{2,1,0:T(8,128)S(1)}, f32[8,128]{1,0:T(8,128)S(1)}) custom-call(s32[3,8192]{1,0:T(4,128)S(1)} %copy-done.1, f32[1,8192]{1,0:T(1,128)S(1)} %bitcast.2), custom_call_target="tpu_custom_call" | custom-call | tf_op jit(solution)/shard_map/pallas_call | solution.py:108
  9.9 31.4 %shard_map.60 = (f32[16,48,512]{2,1,0:T(8,128)S(1)}, f32[12,32,256]{2,1,0:T(8,128)S(1)}, f32[10,32,128]{2,1,0:T(8,128)S(1)}, f32[32,8,128]{2,1,0:T(8,128)S(1)}) custom-call(f32[8,32,512]{2,1,0:T(8,128)S(1)} %get-tuple-element.10.zero, f32[4,16,256]{2,1,0:T(8,128)S(1)} %get-tuple-element.11.one, f32[2,8,128]{2,1,0:T(8,128)S(1)} %get-tuple-element.12.two, ...), custom_call_target="tpu_custom_call" | custom-call | tf_op jit(solution)/shard_map/pallas_call | solution.py:220
  41.3 0.0 copy-start
  41.3 1.1 %copy-done = f32[16,48,512]{2,1,0:T(8,128)} copy-done((f32[16,48,512]{2,1,0:T(8,128)}, f32[16,48,512]{2,1,0:T(8,128)S(1)}, u32[]{:S(2)}) %copy-start) | copy-done | bytes 1572888
  42.5 0.0 copy-start.2
  42.5 0.8 copy-done.2
  43.2 0.0 copy-start.3
  43.2 0.7 copy-done.3
  43.9 0.0 copy-start.5
  43.9 0.7 copy-done.5
  44.6 35.6 %shard_map.61 = (f32[8,32,512]{2,1,0:T(8,128)}, f32[3,8192]{1,0:T(4,128)}) custom-call(s32[3,8192]{1,0:T(4,128)} %cell_ref.3, f32[1,8192]{1,0:T(1,128)} %bitcast.1, f32[16,48,512]{2,1,0:T(8,128)} %copy-done, f32[12,32,256]{2,1,0:T(8,128)} %copy-done.2, f32[10,32,128]{2,1,0:T(8,128)} %copy-done.3, f32[32,8,128]{2,1,0:T(8,128)} %copy-done.5, ...), custom_call_target="tpu_custom_call" | custom-call | tf_op jit(solution)/shard_map/pallas_call | solution.py:483
Async XLA Ops:
  0.6 0.9 %copy-start.1 = (s32[3,8192]{1,0:T(4,128)S(1)}, s32[3,8192]{1,0:T(4,128)}, u32[]{:S(2)}) copy-start(s32[3,8192]{1,0:T(4,128)} %cell_ref.3) | copy-start | bytes 294916
  1.5 0.8 copy-start.4
  41.3 1.1 %copy-start = (f32[16,48,512]{2,1,0:T(8,128)}, f32[16,48,512]{2,1,0:T(8,128)S(1)}, u32[]{:S(2)}) copy-start(f32[16,48,512]{2,1,0:T(8,128)S(1)} %get-tuple-element.14.wide0) | copy-start | bytes 4718596
  42.5 0.8 copy-start.2
  43.2 0.7 copy-start.3
  43.9 0.7 copy-start.5

commit v3 on v2

--- a/solution.py
+++ b/solution.py
@@ -117,11 +117,11 @@
 
 def window(level, dz, dy):
     if level == 0:
-        z = {1: (4, 0, 4), -1: (0, 12, 4), 0: (0, 4, 8)}[dz]
-        y = {1: (24, 0, 8), -1: (0, 40, 8), 0: (0, 8, 32)}[dy]
+        z = {1: (4, 0, 4), -1: (0, 12, 4), 0: (0, 0, 16)}[dz]
+        y = {1: (32, 0, 8), -1: (8, 40, 8), 0: (0, 8, 32)}[dy]
     elif level == 1:
-        z = {1: (0, 0, 4), -1: (0, 8, 4), 0: (0, 4, 4)}[dz]
-        y = {1: (8, 0, 8), -1: (0, 24, 8), 0: (0, 8, 16)}[dy]
+        z = {1: (0, 0, 4), -1: (0, 8, 4), 0: (0, 0, 12)}[dz]
+        y = {1: (16, 0, 8), -1: (8, 24, 8), 0: (0, 8, 16)}[dy]
     else:
         z = (0, 4 - 2 * dz, 2)
         y = (0, 8 - 8 * dy, 8)
@@ -154,8 +154,8 @@
 
     pl.semaphore_wait(barrier, devices - 1)
 
-    offsets = [(0, dz, dy) for dz in (-1, 0, 1) for dy in (-1, 0, 1) if dz or dy]
-    offsets += [(1, dz, dy) for dz in (-1, 0, 1) for dy in (-1, 0, 1) if dz or dy]
+    offsets = [(level, dz, 0) for level in (0, 1) for dz in (-1, 1)]
+    offsets += [(level, 0, dy) for level in (0, 1) for dy in (-1, 1)]
     offsets += [(2, dz, dy) for dz in range(-2, 3) for dy in (-1, 0, 1) if dz or dy]
     sources = (zero, one, two)
     targets = (wide0, wide1, wide2)
@@ -169,7 +169,7 @@
         level, dz, dy = offsets[index]
         (zs, zd, zn), (ys, yd, yn) = window(level, dz, dy)
         return pltpu.make_async_remote_copy(
-            src_ref=sources[level].at[pl.ds(zs, zn), pl.ds(ys, yn), :],
+            src_ref=(targets if level < 2 and dy else sources)[level].at[pl.ds(zs, zn), pl.ds(ys, yn), :],
             dst_ref=targets[level].at[pl.ds(zd, zn), pl.ds(yd, yn), :],
             send_sem=send.at[index],
             recv_sem=recv.at[index],
@@ -187,15 +187,35 @@
             device_id_type=MESH,
         )
 
-    for index, (level, dz, dy) in enumerate(offsets):
-
-        @pl.when(inside(dz, dy))
-        def _():
-            copy_of(index, (slab + dz, pencil + dy)).start()
+    def start(indices):
+        for index in indices:
+            level, dz, dy = offsets[index]
+
+            @pl.when(inside(dz, dy))
+            def _(index=index, dz=dz, dy=dy):
+                copy_of(index, (slab + dz, pencil + dy)).start()
+
+    def finish(indices):
+        for index in indices:
+            level, dz, dy = offsets[index]
+
+            @pl.when(inside(-dz, -dy))
+            def _(index=index, dz=dz, dy=dy):
+                copy_of(index, (slab - dz, pencil - dy)).wait_recv()
+
+            @pl.when(inside(dz, dy))
+            def _(index=index, dz=dz, dy=dy):
+                copy_of(index, (slab + dz, pencil + dy)).wait_send()
+
+    start(range(4))
+    start(range(8, len(offsets)))
 
     @pl.loop(1, devices)
     def _(step):
         top_copy(step, me).start()
+
+    finish(range(4))
+    start(range(4, 8))
 
     @pl.loop(1, devices)
     def _(step):
@@ -203,15 +223,7 @@
         copy.wait_send()
         copy.wait_recv()
 
-    for index, (level, dz, dy) in enumerate(offsets):
-
-        @pl.when(inside(-dz, -dy))
-        def _():
-            copy_of(index, (slab - dz, pencil - dy)).wait_recv()
-
-        @pl.when(inside(dz, dy))
-        def _():
-            copy_of(index, (slab + dz, pencil + dy)).wait_send()
+    finish(range(4, len(offsets)))
 
 
 def exchange_call(slabs, pencils, parts):
@@ -223,8 +235,8 @@
         in_specs=[VMEM] * 4,
         out_specs=[VMEM] * 4,
         scratch_shapes=[
-            pltpu.SemaphoreType.DMA((30,)),
-            pltpu.SemaphoreType.DMA((30,)),
+            pltpu.SemaphoreType.DMA((22,)),
+            pltpu.SemaphoreType.DMA((22,)),
             pltpu.SemaphoreType.DMA((devices,)),
             pltpu.SemaphoreType.DMA((devices,)),
         ],
@@ -498,7 +510,7 @@
             pltpu.VMEM((3 * ROWS, NX), jnp.bfloat16),
             pltpu.VMEM((3 * ROWS, NX), jnp.bfloat16),
         ],
-        compiler_params=pltpu.CompilerParams(vmem_limit_bytes=56 * 2**20),
+        compiler_params=pltpu.CompilerParams(vmem_limit_bytes=24 * 2**20),
     )(
         atom_cell,
         charge.reshape(1, -1),

time: 80.3 us -> 76.9 us (0.958)
  Pallas kernels: 74.6 us -> 71.1 us
    pallas_call x1, Pallas kernels: 35.6 us -> 33.5 us  [field_call(): pl.pallas_call(functools.partial(field_kernel, slabs, pencils), out_shape...]
    pallas_call x1, Pallas kernels: 31.4 us -> 30 us  [exchange_call(): pl.pallas_call(functools.partial(exchange_kernel, slabs, pencils), out_sh...]
    unnamed x12 -> x10, local copies, waits for them, and re-layouts: 4.87 us -> 4.87 us
where the time goes in v3:
time: 76.9 us; the launch traced here: 76.6 us
  Pallas kernels  71.1 us (92%)
  local copies, waits for them, and re-layouts  4.87 us (6%)
    pallas_call x1, Pallas kernels, field_call(): pl.pallas_call(functools.partial(field_kernel, slabs, pencils), out_shape...  33.5 us
    pallas_call x1, Pallas kernels, exchange_call(): pl.pallas_call(functools.partial(exchange_kernel, slabs, pencils), out_sh...  30 us
    pallas_call x1, Pallas kernels, deposit_call(): pl.pallas_call(deposit_kernel, out_shape=[jax.ShapeDtypeStruct(shape, jnp...  7.59 us
    unnamed x10, local copies, waits for them, and re-layouts  4.87 us

profile of v3, /device:TPU:3, one launch (start us, length us, event | category | flops | bytes accessed | tf_op | source)
XLA Modules:
  0.0 76.6 jit_solution(18168674767221420098)
XLA Ops:
  0.6 0.0 copy-start.1
  0.6 0.9 %copy-done.1 = s32[3,8192]{1,0:T(4,128)S(1)} copy-done((s32[3,8192]{1,0:T(4,128)S(1)}, s32[3,8192]{1,0:T(4,128)}, u32[]{:S(2)}) %copy-start.1) | copy-done | bytes 98328
  1.5 0.0 copy-start.4
  1.5 0.8 copy-done.4
  2.3 7.6 %shard_map.59 = (f32[8,32,512]{2,1,0:T(8,128)S(1)}, f32[4,16,256]{2,1,0:T(8,128)S(1)}, f32[2,8,128]{2,1,0:T(8,128)S(1)}, f32[8,128]{1,0:T(8,128)S(1)}) custom-call(s32[3,8192]{1,0:T(4,128)S(1)} %copy-done.1, f32[1,8192]{1,0:T(1,128)S(1)} %bitcast.1), custom_call_target="tpu_custom_call" | custom-call | tf_op jit(solution)/shard_map/pallas_call | solution.py:108
  9.9 30.0 %shard_map.60 = (f32[16,48,512]{2,1,0:T(8,128)S(1)}, f32[12,32,256]{2,1,0:T(8,128)S(1)}, f32[10,32,128]{2,1,0:T(8,128)S(1)}, f32[32,8,128]{2,1,0:T(8,128)S(1)}) custom-call(f32[8,32,512]{2,1,0:T(8,128)S(1)} %get-tuple-element.10.zero, f32[4,16,256]{2,1,0:T(8,128)S(1)} %get-tuple-element.11.one, f32[2,8,128]{2,1,0:T(8,128)S(1)} %get-tuple-element.12.two, ...), custom_call_target="tpu_custom_call" | custom-call | tf_op jit(solution)/shard_map/pallas_call | solution.py:232
  39.9 0.0 copy-start
  39.9 1.3 %copy-done = f32[256,1152]{1,0:T(8,128)S(1)} copy-done((f32[256,1152]{1,0:T(8,128)S(1)}, f32[256,1152]{1,0:T(8,128)}, u32[]{:S(2)}) %copy-start) | copy-done | bytes 1179672
  41.2 0.0 copy-start.2
  41.2 0.9 %copy-done.2 = s32[3,8192]{1,0:T(4,128)S(1)} copy-done((s32[3,8192]{1,0:T(4,128)S(1)}, s32[3,8192]{1,0:T(4,128)}, u32[]{:S(2)}) %copy-start.2) | copy-done | bytes 98328
  42.1 0.0 copy-start.3
  42.1 1.0 %copy-done.3 = f32[128,960]{1,0:T(8,128)S(1)} copy-done((f32[128,960]{1,0:T(8,128)S(1)}, f32[128,960]{1,0:T(8,128)}, u32[]{:S(2)}) %copy-start.3) | copy-done | bytes 491544
  43.1 33.5 %shard_map.61 = (f32[8,32,512]{2,1,0:T(8,128)}, f32[3,8192]{1,0:T(4,128)}) custom-call(s32[3,8192]{1,0:T(4,128)S(1)} %copy-done.2, f32[1,8192]{1,0:T(1,128)S(1)} %bitcast.2, f32[16,48,512]{2,1,0:T(8,128)S(1)} %get-tuple-element.14.wide0, f32[12,32,256]{2,1,0:T(8,128)S(1)} %get-tuple-element.15.wide1, f32[10,32,128]{2,1,0:T(8,128)S(1)} %get-tuple-element.16.wide2, ...), custom_call_target="tpu_custom_call" | custom-call | tf_op jit(solution)/shard_map/pallas_call | solution.py:495
Async XLA Ops:
  0.6 0.9 %copy-start.1 = (s32[3,8192]{1,0:T(4,128)S(1)}, s32[3,8192]{1,0:T(4,128)}, u32[]{:S(2)}) copy-start(s32[3,8192]{1,0:T(4,128)} %cell_ref.3) | copy-start | bytes 294916
  1.5 0.8 copy-start.4
  39.9 1.3 %copy-start = (f32[256,1152]{1,0:T(8,128)S(1)}, f32[256,1152]{1,0:T(8,128)}, u32[]{:S(2)}) copy-start(f32[256,1152]{1,0:T(8,128)} %constant.4.clone.stencil1) | copy-start | bytes 3538948
  41.2 0.9 %copy-start.2 = (s32[3,8192]{1,0:T(4,128)S(1)}, s32[3,8192]{1,0:T(4,128)}, u32[]{:S(2)}) copy-start(s32[3,8192]{1,0:T(4,128)} %cell_ref.3) | copy-start | bytes 294916
  42.1 1.0 %copy-start.3 = (f32[128,960]{1,0:T(8,128)S(1)}, f32[128,960]{1,0:T(8,128)}, u32[]{:S(2)}) copy-start(f32[128,960]{1,0:T(8,128)} %constant.5.clone.stencil2) | copy-start | bytes 1474564

commit v4 on v3

--- a/solution.py
+++ b/solution.py
@@ -16,7 +16,6 @@
 ROWS = CZ * CY
 CHUNK = 1024
 MESH = pl.DeviceIdType.MESH
-HIGHEST = lax.Precision.HIGHEST
 VMEM = pl.BlockSpec(memory_space=pltpu.VMEM)
 SQUARES = (0, 1, 2, 4, 5, 8)
 
@@ -31,15 +30,19 @@
 
 def level_weight(level, squared):
     return (1.0 / math.sqrt(squared + 1.0) - 1.0 / math.sqrt(squared + 4.0)) / 2**level
-
-
-def dot32(left, right):
-    return jnp.dot(left, right, precision=HIGHEST, preferred_element_type=jnp.float32)
 
 
 def split_two(values):
     high = values.astype(jnp.bfloat16)
     return high, (values - high.astype(jnp.float32)).astype(jnp.bfloat16)
+
+
+def dot32(left, right):
+    left_high, left_low = split_two(left)
+    right_high, right_low = split_two(right)
+    total = jnp.dot(left_high, right_high, preferred_element_type=jnp.float32)
+    total += jnp.dot(left_high, right_low, preferred_element_type=jnp.float32)
+    return total + jnp.dot(left_low, right_high, preferred_element_type=jnp.float32)
 
 
 def local_rows(cell_ref, start, width):

time: 76.9 us -> 74.7 us (0.971)
  Pallas kernels: 71.1 us -> 68.9 us
    pallas_call x1, Pallas kernels: 33.5 us -> 31.7 us  [field_call(): pl.pallas_call(functools.partial(field_kernel, slabs, pencils), out_shape...]
where the time goes in v4:
time: 74.7 us; the launch traced here: 74.4 us
  Pallas kernels  68.9 us (92%)
  local copies, waits for them, and re-layouts  4.87 us (7%)
    pallas_call x1, Pallas kernels, field_call(): pl.pallas_call(functools.partial(field_kernel, slabs, pencils), out_shape...  31.7 us
    pallas_call x1, Pallas kernels, exchange_call(): pl.pallas_call(functools.partial(exchange_kernel, slabs, pencils), out_sh...  30 us
    pallas_call x1, Pallas kernels, deposit_call(): pl.pallas_call(deposit_kernel, out_shape=[jax.ShapeDtypeStruct(shape, jnp...  7.17 us
    unnamed x10, local copies, waits for them, and re-layouts  4.87 us

profile of v4, /device:TPU:3, one launch (start us, length us, event | category | flops | bytes accessed | tf_op | source)
XLA Modules:
  0.0 74.4 jit_solution(17901174591567538883)
XLA Ops:
  0.6 0.0 copy-start.1
  0.6 0.9 %copy-done.1 = s32[3,8192]{1,0:T(4,128)S(1)} copy-done((s32[3,8192]{1,0:T(4,128)S(1)}, s32[3,8192]{1,0:T(4,128)}, u32[]{:S(2)}) %copy-start.1) | copy-done | bytes 98328
  1.5 0.0 copy-start.4
  1.5 0.8 %copy-done.4 = f32[8192]{0:T(1024)S(1)} copy-done((f32[8192]{0:T(1024)S(1)}, f32[8192]{0:T(1024)}, u32[]{:S(2)}) %copy-start.4) | copy-done | bytes 32792
  2.3 7.2 %shard_map.59 = (f32[8,32,512]{2,1,0:T(8,128)S(1)}, f32[4,16,256]{2,1,0:T(8,128)S(1)}, f32[2,8,128]{2,1,0:T(8,128)S(1)}, f32[8,128]{1,0:T(8,128)S(1)}) custom-call(s32[3,8192]{1,0:T(4,128)S(1)} %copy-done.1, f32[1,8192]{1,0:T(1,128)S(1)} %bitcast.1), custom_call_target="tpu_custom_call" | custom-call | tf_op jit(solution)/shard_map/pallas_call | solution.py:111
  9.5 30.0 %shard_map.60 = (f32[16,48,512]{2,1,0:T(8,128)S(1)}, f32[12,32,256]{2,1,0:T(8,128)S(1)}, f32[10,32,128]{2,1,0:T(8,128)S(1)}, f32[32,8,128]{2,1,0:T(8,128)S(1)}) custom-call(f32[8,32,512]{2,1,0:T(8,128)S(1)} %get-tuple-element.10.zero, f32[4,16,256]{2,1,0:T(8,128)S(1)} %get-tuple-element.11.one, f32[2,8,128]{2,1,0:T(8,128)S(1)} %get-tuple-element.12.two, ...), custom_call_target="tpu_custom_call" | custom-call | tf_op jit(solution)/shard_map/pallas_call | solution.py:235
  39.5 0.0 copy-start
  39.5 1.3 %copy-done = f32[256,1152]{1,0:T(8,128)S(1)} copy-done((f32[256,1152]{1,0:T(8,128)S(1)}, f32[256,1152]{1,0:T(8,128)}, u32[]{:S(2)}) %copy-start) | copy-done | bytes 1179672
  40.7 0.0 copy-start.2
  40.7 0.9 %copy-done.2 = s32[3,8192]{1,0:T(4,128)S(1)} copy-done((s32[3,8192]{1,0:T(4,128)S(1)}, s32[3,8192]{1,0:T(4,128)}, u32[]{:S(2)}) %copy-start.2) | copy-done | bytes 98328
  41.6 0.0 copy-start.3
  41.6 1.0 %copy-done.3 = f32[128,960]{1,0:T(8,128)S(1)} copy-done((f32[128,960]{1,0:T(8,128)S(1)}, f32[128,960]{1,0:T(8,128)}, u32[]{:S(2)}) %copy-start.3) | copy-done | bytes 491544
  42.7 31.7 %shard_map.61 = (f32[8,32,512]{2,1,0:T(8,128)}, f32[3,8192]{1,0:T(4,128)}) custom-call(s32[3,8192]{1,0:T(4,128)S(1)} %copy-done.2, f32[1,8192]{1,0:T(1,128)S(1)} %bitcast.2, f32[16,48,512]{2,1,0:T(8,128)S(1)} %get-tuple-element.14.wide0, f32[12,32,256]{2,1,0:T(8,128)S(1)} %get-tuple-element.15.wide1, f32[10,32,128]{2,1,0:T(8,128)S(1)} %get-tuple-element.16.wide2, ...), custom_call_target="tpu_custom_call" | custom-call | tf_op jit(solution)/shard_map/pallas_call | solution.py:498
Async XLA Ops:
  0.6 0.9 %copy-start.1 = (s32[3,8192]{1,0:T(4,128)S(1)}, s32[3,8192]{1,0:T(4,128)}, u32[]{:S(2)}) copy-start(s32[3,8192]{1,0:T(4,128)} %cell_ref.3) | copy-start | bytes 294916
  1.5 0.8 %copy-start.4 = (f32[8192]{0:T(1024)S(1)}, f32[8192]{0:T(1024)}, u32[]{:S(2)}) copy-start(f32[8192]{0:T(1024)} %param.5) | copy-start | bytes 98308
  39.5 1.3 %copy-start = (f32[256,1152]{1,0:T(8,128)S(1)}, f32[256,1152]{1,0:T(8,128)}, u32[]{:S(2)}) copy-start(f32[256,1152]{1,0:T(8,128)} %constant.4.clone.stencil1) | copy-start | bytes 3538948
  40.7 0.9 %copy-start.2 = (s32[3,8192]{1,0:T(4,128)S(1)}, s32[3,8192]{1,0:T(4,128)}, u32[]{:S(2)}) copy-start(s32[3,8192]{1,0:T(4,128)} %cell_ref.3) | copy-start | bytes 294916
  41.6 1.0 %copy-start.3 = (f32[128,960]{1,0:T(8,128)S(1)}, f32[128,960]{1,0:T(8,128)}, u32[]{:S(2)}) copy-start(f32[128,960]{1,0:T(8,128)} %constant.5.clone.stencil2) | copy-start | bytes 1474564
